TPU v7x, 32 devices: a whole 2x2x4 slice. The times are simulated.
32 devices in a mesh: groups: 2 (over y), frame: 4 (over z), row: 2 (over core), head: 2 (over x).
Axes of the slice: x: 2, y: 2, z: 4, core: 2. Of those that a mesh axis runs over, the one named last changes fastest.
Arguments:
- queries: bfloat16 [8, 16, 48, 768], P(('groups', 'frame'), 'row', None, 'head'), parts along dimension 0, may hold values from -8 to 8
- keys: bfloat16 [8, 16, 48, 768], P(('groups', 'frame'), 'row', None, 'head'), parts along dimension 0, may hold values from -8 to 8
- values: bfloat16 [8, 16, 48, 768], P(('groups', 'frame'), 'row', None, 'head'), parts along dimension 0, may hold values from -6 to 6
- valid_prev: int32 [8, 16], P(('groups', 'frame'), 'row'), parts along dimension 0, may hold values 0 or 1
- mem_index: int32 [4], P('groups'), parts along dimension 0, may hold values from 0 to 3
Outputs:
- attended: bfloat16 [8, 16, 48, 768], P(('groups', 'frame'), 'row', None, 'head'), parts along dimension 0
There are 2 independent parts, one for each index of `groups`. A program takes and returns all parts, laid end to end along the dimension named above; each array names one. Nothing has to cross between parts.
All inputs are finite; a program needn't handle non-finite values. No bound on the sum of `valid_prev` on one device may be relied on, other than what follows from the above.
Results may differ from a plain program's by a relative error of at most 0.0085.
Values may be sent and summed in bfloat16 or wider, within the bound.
No kernel may reach another device: no remote copies, remote signals or barrier semaphores. Data moves between devices by JAX's collectives and lax.ppermute only.
A program may use at most 128 MiB of HBM per device.

v0:
```python
import jax
import jax.numpy as jnp
from jax import lax
from jax.sharding import PartitionSpec as P

HEAD_DIM = 128
WINDOW = 2


def passed_along(block, axis, distance):
    devices = range(lax.axis_size(axis))
    route = [(i - distance, i) for i in devices if i - distance in devices]
    return lax.ppermute(block, axis, route)


def on_device(queries, keys, values, valid_prev, mem_index):
    rows_dev = queries.shape[1]
    frame_width = queries.shape[2]
    channels = queries.shape[3]
    head_count = channels // HEAD_DIM
    n_rows = lax.axis_size("row")
    band_index = lax.axis_index("row")
    frame_index = lax.axis_index("frame")
    frame_rows = rows_dev * n_rows
    key_value = jnp.stack([keys[0], values[0]])
    masked = jnp.stack(
        [
            jnp.where(frame_index == mem_index[memory_slot], key_value.astype(jnp.float32), 0.0)
            for memory_slot in range(2)
        ]
    )
    summed = lax.psum(masked.astype(jnp.bfloat16), "frame")
    memory_bands = [summed[0], summed[1]]
    collected = lax.all_gather(
        jnp.stack([key_value, memory_bands[0], memory_bands[1]]), "row", axis=2, tiled=True
    )
    own_frame = collected[0]
    memory = collected[1:]
    shifted = passed_along(own_frame, "frame", 1)
    padded = jnp.pad(shifted, ((0, 0), (WINDOW, WINDOW), (0, 0), (0, 0)))
    previous = lax.dynamic_slice_in_dim(padded, band_index * rows_dev, rows_dev + 2 * WINDOW, 1)
    query_count = rows_dev * frame_width
    query_rows = band_index * rows_dev + jnp.arange(query_count, dtype=jnp.int32) // frame_width
    key_rows = (
        band_index * rows_dev
        - WINDOW
        + jnp.arange((rows_dev + 2 * WINDOW) * frame_width, dtype=jnp.int32) // frame_width
    )
    row_valid = jnp.broadcast_to((valid_prev[0] > 0)[:, None], (rows_dev, frame_width)).reshape(
        query_count
    )
    usable = row_valid & (frame_index > 0)
    near_rows = (
        (jnp.abs(key_rows[None, :] - query_rows[:, None]) <= WINDOW)
        & ((key_rows >= 0) & (key_rows < frame_rows))[None, :]
        & usable[:, None]
    )
    frame_tokens = frame_rows * frame_width
    allowed = jnp.concatenate(
        [
            jnp.ones((query_count, frame_tokens), dtype=bool),
            near_rows,
            jnp.ones((query_count, 2 * frame_tokens), dtype=bool),
        ],
        1,
    )

    def flatten(array):
        return array.reshape(-1, head_count, HEAD_DIM)

    all_keys = jnp.concatenate(
        [flatten(own_frame[0]), flatten(previous[0]), flatten(memory[0, 0]), flatten(memory[1, 0])],
        0,
    )
    all_values = jnp.concatenate(
        [flatten(own_frame[1]), flatten(previous[1]), flatten(memory[0, 1]), flatten(memory[1, 1])],
        0,
    )
    query_heads = queries[0].reshape(query_count, head_count, HEAD_DIM)

    def one_head(operands):
        head_queries, head_keys, head_values = operands
        scores = jnp.einsum(
            "qd,kd->qk", head_queries, head_keys, preferred_element_type=jnp.float32
        ) * HEAD_DIM ** (-0.5)
        scores = jnp.where(allowed, scores, -jnp.inf)
        peak = jnp.max(scores, axis=1, keepdims=True)
        total = jnp.sum(jnp.exp(scores - peak), axis=1, keepdims=True)
        weights = (jnp.exp(scores - peak) / total).astype(jnp.bfloat16)
        return jnp.einsum("qk,kd->qd", weights, head_values, preferred_element_type=jnp.float32)

    result = lax.map(
        one_head,
        (
            jnp.transpose(query_heads, (1, 0, 2)),
            jnp.transpose(all_keys, (1, 0, 2)),
            jnp.transpose(all_values, (1, 0, 2)),
        ),
    )
    result = jnp.transpose(result, (1, 0, 2))
    return result.reshape(queries.shape).astype(jnp.bfloat16)


def solution(mesh):
    placed = (
        P(("groups", "frame"), "row", None, "head"),
        P(("groups", "frame"), "row", None, "head"),
        P(("groups", "frame"), "row", None, "head"),
        P(("groups", "frame"), "row"),
        P("groups"),
    )
    return jax.shard_map(
        on_device,
        mesh=mesh,
        in_specs=placed,
        out_specs=P(("groups", "frame"), "row", None, "head"),
        check_vma=False,
    )
```

profile of v0, /device:TPU:0, one launch (start us, length us, event | category | flops | bytes accessed | tf_op | source)
XLA Modules:
  0.0 190.8 jit_solution(14923785144539808250)
XLA Ops:
  6.5 1.4 fusion.27
  9.2 1.2 fusion.13
  10.4 1.2 pad_maximum_fusion.1
  11.8 58.6 %all-reduce.3.cloned.1.call-done = bf16[2,2,8,48,384]{4,3,2,1,0:T(8,128)(2,1)} async-done(((bf16[2,2,8,48,384]{4,3,2,1,0:T(8,128)(2,1)}), bf16[2,2,8,48,384]{4,3,2,1,0:T(8,128)(2,1)}) %all-reduce.3.cloned.1.call-update) | async-done | bytes 1179664 | tf_op jit(solution)/shard_map/psum | solution.py:32
  70.4 2.7 %pad_maximum_fusion = bf16[3,2,8,48,384]{4,3,2,1,0:T(8,128)(2,1)} fusion(bf16[2,2,8,48,384]{4,3,2,1,0:T(8,128)(2,1)} %all-reduce.3.cloned.1.call-done, bf16[1,2,8,48,384]{4,3,2,1,0:T(8,128)(2,1)S(1)} %maximum_bitcast_fusion.2), kind=kLoop, calls=%fused_computation.19 | loop fusion | flops 884736 | bytes 3538944 | tf_op jit(solution)/shard_map/stack | solution.py:35
  73.5 0.8 copy.7
  74.3 11.2 %all-gather.2.cloned.1.call-done = bf16[3,2,16,48,384]{4,3,2,1,0:T(8,128)(2,1)} async-done(((bf16[3,2,8,48,384]{4,3,2,1,0:T(8,128)(2,1)}), bf16[3,2,16,48,384]{4,3,2,1,0:T(8,128)(2,1)}) %all-gather.2.cloned.1.call-update) | async-done | bytes 3538960 | tf_op jit(solution)/shard_map/all_gather | solution.py:34
  85.5 2.6 %slice_bitcast_fusion = bf16[2,16,48,384]{3,2,1,0:T(8,128)(2,1)} fusion(bf16[3,2,16,48,384]{4,3,2,1,0:T(8,128)(2,1)} %all-gather.2.cloned.1.call-done), kind=kLoop, calls=%fused_computation.26 | loop fusion | bytes 2359296 | tf_op jit(solution)/shard_map/squeeze | solution.py:37
  88.1 4.7 %collective-permute-start = (bf16[2,16,48,384]{3,2,1,0:T(8,128)(2,1)}, bf16[2,16,48,384]{3,2,1,0:T(8,128)(2,1)}, u32[]{:S(2)}, u32[]{:S(2)}) collective-permute-start(bf16[2,16,48,384]{3,2,1,0:T(8,128)(2,1)} %slice_bitcast_fusion), channel_id=1, source_target_pairs={{0,4},{4,8},{8,12},{1,5},{5,9},{9,13},{2,6},{6,10},{10,14},{3,7},{... | collective-permute-start | bytes 3538952 | tf_op jit(solution)/shard_map/ppermute | solution.py:13
  93.2 2.6 %add_add_fusion = pred[384,2880]{0,1:T(32,128)(4,1)S(1)} fusion(pred[384,576]{0,1:T(32,128)(4,1)S(1)} %fusion.16, pred[2880]{0:T(1024)(128)(4,1)S(1)} %pad.11.clone, pred[2880]{0:T(1024)(128)(4,1)S(1)} %pad.9.clone), kind=kLoop, calls=%fused_computation.16 | loop fusion | flops 2211840 | bytes 1332864 | tf_op jit(solution)/shard_map/concatenate | solution.py:59
  95.8 1.4 fusion.26
  97.2 2.6 %reshape_squeeze.32 = bf16[768,3,128]{2,1,0:T(4,128)(2,1)} reshape(bf16[1,1,16,48,384]{4,3,2,1,0:T(8,128)(2,1)} %get-tuple-element.58) | data formatting | bytes 1179648 | tf_op jit(solution)/shard_map/reshape;squeeze | solution.py:69
  99.8 2.6 %reshape_squeeze.34 = bf16[768,3,128]{2,1,0:T(4,128)(2,1)} reshape(bf16[1,1,16,48,384]{4,3,2,1,0:T(8,128)(2,1)} %get-tuple-element.60) | data formatting | bytes 1179648 | tf_op jit(solution)/shard_map/reshape;squeeze | solution.py:69
  102.5 1.0 reshape_squeeze.35
  103.8 2.0 %reshape_squeeze.31 = bf16[768,3,128]{2,1,0:T(4,128)(2,1)S(1)} reshape(bf16[1,1,16,48,384]{4,3,2,1,0:T(8,128)(2,1)} %get-tuple-element.61) | data formatting | bytes 1179648 | tf_op jit(solution)/shard_map/reshape;squeeze | solution.py:69
  105.8 11.9 %collective-permute-done = bf16[2,16,48,384]{3,2,1,0:T(8,128)(2,1)} collective-permute-done((bf16[2,16,48,384]{3,2,1,0:T(8,128)(2,1)}, bf16[2,16,48,384]{3,2,1,0:T(8,128)(2,1)}, u32[]{:S(2)}, u32[]{:S(2)}) %collective-permute-start) | collective-permute-done | bytes 1179680 | tf_op jit(solution)/shard_map/ppermute | solution.py:13
  117.8 2.1 %pad_dynamic-slice_fusion.1 = (bf16[1,12,48,384]{3,2,1,0:T(8,128)(2,1)}, bf16[1,12,48,384]{3,2,1,0:T(8,128)(2,1)}) fusion(s32[]{:T(128)S(6)} %add.54, s32[]{:T(128)S(6)} %select_n.60, bf16[2,16,48,384]{3,2,1,0:T(8,128)(2,1)} %collective-permute-done), kind=kLoop, calls=%fused_computation.23 | loop fusion | bytes 2064392 | tf_op jit(solution)/shard_map/slice | solution.py:76
  119.9 2.1 %reshape_squeeze.33 = bf16[576,3,128]{2,1,0:T(4,128)(2,1)} reshape(bf16[1,12,48,384]{3,2,1,0:T(8,128)(2,1)} %get-tuple-element.64) | data formatting | bytes 884736 | tf_op jit(solution)/shard_map/reshape;squeeze | solution.py:69
  122.0 10.6 %maximum_bitcast_fusion.1 = bf16[3,2880,128]{2,0,1:T(4,128)(2,1)S(1)} fusion(bf16[768,3,128]{2,1,0:T(4,128)(2,1)} %reshape_squeeze.35, bf16[768,3,128]{2,1,0:T(4,128)(2,1)} %reshape_squeeze.34, bf16[576,3,128]{2,1,0:T(4,128)(2,1)} %reshape_squeeze.33, bf16[768,3,128]{2,1,0:T(4,128)(2,1)} %reshape_squeeze.32), kind=kLoop, calls=%fused_computation.18 | loop fusion | flops 3317760 | bytes 4423680 | tf_op jit(solution)/shard_map/transpose | solution.py:97
  132.6 1.7 copy.9
  134.3 2.1 %reshape_squeeze.29 = bf16[576,3,128]{2,1,0:T(4,128)(2,1)} reshape(bf16[1,12,48,384]{3,2,1,0:T(8,128)(2,1)} %get-tuple-element.65) | data formatting | bytes 884736 | tf_op jit(solution)/shard_map/reshape;squeeze | solution.py:69
  136.4 29.2 %maximum_bitcast_fusion = bf16[3,2880,128]{2,0,1:T(4,128)(2,1)S(1)} fusion(bf16[768,3,128]{2,1,0:T(4,128)(2,1)S(1)} %reshape_squeeze.31, bf16[768,3,128]{2,1,0:T(4,128)(2,1)S(1)} %reshape_squeeze.30, bf16[576,3,128]{2,1,0:T(4,128)(2,1)} %reshape_squeeze.29, bf16[768,3,128]{2,1,0:T(4,128)(2,1)S(1)} %reshape_squeeze.28), kind=kLoop, calls=%fused_computation.17 | loop fusion | flops 3317760 | bytes 4423680 | tf_op jit(solution)/shard_map/transpose | solution.py:96
  165.9 15.9 %while.10 = (s32[]{:T(128)}, bf16[3,384,128]{2,1,0:T(8,128)(2,1)}, bf16[3,384,128]{2,1,0:T(8,128)(2,1)}, bf16[3,2880,128]{2,1,0:T(8,128)(2,1)S(1)}, pred[384,288...) while((s32[]{:T(128)}, bf16[3,384,128]{2,1,0:T(8,128)(2,1)}, ...), condition=%wide.region_4.5_spmd, body=%wide.region_1.4_spmd.sunk | while | flops 575077632 | bytes 16156237 | solution.py:92
  166.1 1.8 fusion.33
  168.0 0.7 fusion.34
  168.7 2.7 %fusion.35 = bf16[3,384,128]{2,1,0:T(8,128)(2,1)} fusion(bf16[3,384,128]{2,1,0:T(8,128)(2,1)} %get-tuple-element.119, s32[]{:T(128)} %get-tuple-element.118, f32[384,2880]{0,1:T(8,128)S(1)} %get-tuple-element.109, f32[384]{0:T(512)S(1)} %fusion.34, f32[384]{0:T(512)S(1)} %get-tuple-element.110, bf16[3,2880,128]{2,1,0:T(8,128)(2,1)} %get-tuple-element.130), kind=kOutput, calls=%fused_computation.7.clone.1 | convolution fusion | flops 286433280 | bytes 5361664 | tf_op jit(solution)/shard_map/while/body/eval_jaxpr/qk,kd->qd/dot_general | solution.py:90
  171.4 1.8 fusion.33
  173.9 2.7 %fusion.35 = bf16[3,384,128]{2,1,0:T(8,128)(2,1)} fusion(bf16[3,384,128]{2,1,0:T(8,128)(2,1)} %get-tuple-element.119, s32[]{:T(128)} %get-tuple-element.118, f32[384,2880]{0,1:T(8,128)S(1)} %get-tuple-element.109, f32[384]{0:T(512)S(1)} %fusion.34, f32[384]{0:T(512)S(1)} %get-tuple-element.110, bf16[3,2880,128]{2,1,0:T(8,128)(2,1)} %get-tuple-element.130), kind=kOutput, calls=%fused_computation.7.clone.1 | convolution fusion | flops 286433280 | bytes 5361664 | tf_op jit(solution)/shard_map/while/body/eval_jaxpr/qk,kd->qd/dot_general | solution.py:90
  176.6 1.8 fusion.33
  179.1 2.7 %fusion.35 = bf16[3,384,128]{2,1,0:T(8,128)(2,1)} fusion(bf16[3,384,128]{2,1,0:T(8,128)(2,1)} %get-tuple-element.119, s32[]{:T(128)} %get-tuple-element.118, f32[384,2880]{0,1:T(8,128)S(1)} %get-tuple-element.109, f32[384]{0:T(512)S(1)} %fusion.34, f32[384]{0:T(512)S(1)} %get-tuple-element.110, bf16[3,2880,128]{2,1,0:T(8,128)(2,1)} %get-tuple-element.130), kind=kOutput, calls=%fused_computation.7.clone.1 | convolution fusion | flops 286433280 | bytes 5361664 | tf_op jit(solution)/shard_map/while/body/eval_jaxpr/qk,kd->qd/dot_general | solution.py:90
  181.8 1.2 copy.10
  183.0 1.0 convert_element_type.41
  (33 shorter events, 3.1 us)
Async XLA Ops:
  6.5 63.9 %all-reduce.3.cloned.1.call-start = ((), (), s32[]{:S(2)}) async-start(), calls=%async_computation | async-start | bytes 2359296 | tf_op jit(solution)/shard_map/psum | solution.py:32
  10.4 1.3 copy-start.1
  10.4 1.3 copy-start.2
  11.6 73.9 %all-gather.2.cloned.1.call-start = ((), (), s32[]{:S(2)}) async-start(), calls=%async_computation.1 | async-start | bytes 5308416 | tf_op jit(solution)/shard_map/all_gather | solution.py:34
  11.8 61.3 %copy-start.4 = (s32[1,8]{1,0:T(1,128)S(1)}, s32[1,8]{1,0:T(1,128)}, u32[]{:S(2)}) copy-start(s32[1,8]{1,0:T(1,128)} %param.10) | copy-start | bytes 100
  11.8 61.6 %copy-start.3 = (bf16[1,8,48,384]{3,2,1,0:T(8,128)(2,1)S(1)}, bf16[1,8,48,384]{3,2,1,0:T(8,128)(2,1)}, u32[]{:S(2)}) copy-start(bf16[1,8,48,384]{3,2,1,0:T(8,128)(2,1)} %param.7) | copy-start | bytes 884740
  85.5 10.3 %copy-start = (bf16[3,2,16,48,384]{4,3,2,1,0:T(8,128)(2,1)S(1)}, bf16[3,2,16,48,384]{4,3,2,1,0:T(8,128)(2,1)}, u32[]{:S(2)}) copy-start(bf16[3,2,16,48,384]{4,3,2,1,0:T(8,128)(2,1)} %all-gather.2.cloned.1.call-done) | copy-start | bytes 10616836
  88.1 29.6 %collective-permute-start = (bf16[2,16,48,384]{3,2,1,0:T(8,128)(2,1)}, bf16[2,16,48,384]{3,2,1,0:T(8,128)(2,1)}, u32[]{:S(2)}, u32[]{:S(2)}) collective-permute-start(bf16[2,16,48,384]{3,2,1,0:T(8,128)(2,1)} %slice_bitcast_fusion), channel_id=1, source_target_pairs={{0,4},{4,8},{8,12},{1,5},{5,9},{9,13},{2,6},{6,10},{10,14},{3,7},{... | collective-permute-start | bytes 3538952 | tf_op jit(solution)/shard_map/ppermute | solution.py:13
Sparse Core Ops, SparseCore 0:
  11.8 58.5 all-reduce.2
  73.2 12.2 all-gather.1
where the time goes:
time: 192 us; the launch traced here: 191 us
  waiting for transfers between devices  81.7 us (43%)
  other arithmetic  50.1 us (26%)
  local copies, waits for them, and re-layouts  25.6 us (13%)
  between operations  14.9 us (8%)
  matrix products  13.4 us (7%)
  starting transfers between devices  4.73 us (2%)
    psum x1, waiting for transfers between devices, on_device(): summed = lax.psum(masked.astype(jnp.bfloat16), 'frame')  58.6 us
    transpose x1, other arithmetic, on_device(): jnp.transpose(all_keys, (1, 0, 2))  29.2 us
    another operation x8, local copies, waits for them, and re-layouts, flatten(): return array.reshape(-1, head_count, HEAD_DIM)  12.8 us
    ppermute x1, waiting for transfers between devices, passed_along(): return lax.ppermute(block, axis, route)  11.9 us
    all_gather x1, waiting for transfers between devices, on_device(): lax.all_gather(jnp.stack([key_value, memory_bands[0], memory_bands[1]]),...  11.2 us
    transpose x1, other arithmetic, on_device(): jnp.transpose(all_values, (1, 0, 2))  10.6 us
    dot_general x3, matrix products, one_head(): jnp.einsum('qk,kd->qd', weights, head_values, preferred_element_type=jnp....  7.98 us
    dot_general x3, matrix products, one_head(): jnp.einsum('qd,kd->qk', head_queries, head_keys, preferred_element_type=j...  5.47 us
  transfers between devices with their start and end apart: 3, of which 3 were waited for; matrix products, arithmetic and copies ran while one was open for 7% of the time, Pallas kernels for 0%

commit v1 on v0

v1 whole, which is shorter than its diff:
```python
import functools

import jax
import jax.numpy as jnp
from jax import lax
from jax.experimental import pallas as pl
from jax.experimental.pallas import tpu as pltpu
from jax.sharding import PartitionSpec as P

HEAD_DIM = 128
WINDOW = 2
SCALE = HEAD_DIM**-0.5 * 1.4426950408889634
FLOOR = -1e30
BLOCK = 128


def moved(block, axis, pairs):
    return lax.ppermute(block, axis, pairs)


def swapped(block):
    return lax.ppermute(block, "row", [(0, 1), (1, 0)])


def row_dot(a, b):
    return lax.dot_general(a, b, (((1,), (1,)), ((), ())), preferred_element_type=jnp.float32)


def attend_kernel(plan, n_q, n_f, fresh, finish, width, *refs):
    refs = list(refs)
    mem_ref = refs.pop(0)
    valid_refs = [refs.pop(0) for _ in range(n_q)]
    q_refs = [refs.pop(0) for _ in range(n_q)]
    frames = [[refs.pop(0) for _ in range(4)] for _ in range(n_f)]
    states = [None if fresh[i] else (refs.pop(0), refs.pop(0)) for i in range(n_q)]
    outs = [(refs.pop(0),) if finish[i] else (refs.pop(0), refs.pop(0)) for i in range(n_q)]
    acc, stat = refs
    queries = q_refs[0].shape[0]
    rows = queries // width
    band = lax.axis_index("row")
    lane = lax.broadcasted_iota(jnp.int32, (1, HEAD_DIM), 1)

    for i in range(n_q):
        if fresh[i]:
            acc[i] = jnp.zeros_like(acc[i])
            stat[i] = jnp.where(lane == 0, FLOOR, jnp.zeros_like(stat[i]))
        else:
            acc[i] = states[i][0][...]
            stat[i] = states[i][1][...]

    def step(i, f, times, window):
        key_a, value_a, key_b, value_b = frames[f]
        factor = times.astype(jnp.float32)
        for start in range(0, queries, BLOCK):
            part = pl.ds(start, BLOCK)
            query = q_refs[i][part, :]
            scores = [row_dot(query, key[...]) * SCALE for key in (key_a, key_b)]
            if window:
                place = lax.broadcasted_iota(jnp.int32, (BLOCK, 1), 0) + start
                row = jnp.full((BLOCK, 1), -1000, jnp.int32)
                for r in range(rows):
                    here = jnp.where(valid_refs[i][0, r] > 0, band * rows + r, -1000)
                    row = jnp.where((place >= r * width) & (place < (r + 1) * width), here, row)
                place = lax.broadcasted_iota(jnp.int32, (1, queries), 1)
                key_row = jnp.zeros((1, queries), jnp.int32)
                for r in range(1, rows):
                    key_row = key_row + (place >= r * width).astype(jnp.int32)
                near = [
                    jnp.abs(key_row + half * rows - row) <= WINDOW for half in (band, 1 - band)
                ]
                weight = [jnp.where(n, factor + 1.0, factor) for n in near]
                scores = [jnp.where(w > 0.0, s, -jnp.inf) for s, w in zip(scores, weight)]
            old = stat[i, part, 0:1]
            total = stat[i, part, 1:2]
            peak = jnp.maximum(
                jnp.max(scores[0], axis=1, keepdims=True), jnp.max(scores[1], axis=1, keepdims=True)
            )
            peak = jnp.maximum(old, peak)
            terms = [jnp.exp2(s - peak) for s in scores]
            if window:
                terms = [t * w for t, w in zip(terms, weight)]
            added = jnp.sum(terms[0], axis=1, keepdims=True) + jnp.sum(
                terms[1], axis=1, keepdims=True
            )
            mixed = sum(
                jnp.dot(t.astype(jnp.bfloat16), v[...], preferred_element_type=jnp.float32)
                for t, v in zip(terms, (value_a, value_b))
            )
            if not window:
                added = added * factor
                mixed = mixed * factor
            fade = jnp.exp2(old - peak)
            acc[i, part, :] = acc[i, part, :] * fade + mixed
            stat[i, part, :] = jnp.where(lane == 0, peak, total * fade + added)

    z = lax.axis_index("frame")
    for i in range(n_q):
        for f in range(n_f):
            wanted = plan(z, mem_ref[0], mem_ref[1], i, f)
            if wanted is None:
                continue
            times, window = wanted
            if window is None:
                pl.when(times > 0)(functools.partial(step, i, f, times, False))
            else:
                pl.when(window)(functools.partial(step, i, f, times, True))
                pl.when((times > 0) & jnp.logical_not(window))(
                    functools.partial(step, i, f, times, False)
                )

    for i in range(n_q):
        if finish[i]:
            outs[i][0][...] = (acc[i] / stat[i, :, 1:2]).astype(jnp.bfloat16)
        else:
            outs[i][0][...] = acc[i]
            outs[i][1][...] = stat[i]


def attend(plan, mem_index, valids, queries, frames, states, finish, width):
    n_q, n_f = len(queries), len(frames)
    tokens, channels = queries[0].shape
    heads = channels // HEAD_DIM
    block = pl.BlockSpec((tokens, HEAD_DIM), lambda h: (0, h))
    scalars = pl.BlockSpec(memory_space=pltpu.SMEM)
    fresh = tuple(s is None for s in states)
    operands = [mem_index, *valids, *queries]
    specs = [scalars] * (1 + n_q) + [block] * n_q
    for frame in frames:
        operands += frame
        specs += [block] * 4
    for state in states:
        if state is not None:
            operands += state
            specs += [block] * 2
    shapes = []
    for done in finish:
        if done:
            shapes.append(jax.ShapeDtypeStruct((tokens, channels), jnp.bfloat16))
        else:
            shapes += [jax.ShapeDtypeStruct((tokens, channels), jnp.float32)] * 2
    outs = pl.pallas_call(
        functools.partial(attend_kernel, plan, n_q, n_f, fresh, tuple(finish), width),
        grid=(heads,),
        in_specs=specs,
        out_specs=[block] * len(shapes),
        out_shape=shapes,
        scratch_shapes=[
            pltpu.VMEM((n_q, tokens, HEAD_DIM), jnp.float32),
            pltpu.VMEM((n_q, tokens, HEAD_DIM), jnp.float32),
        ],
        compiler_params=pltpu.CompilerParams(vmem_limit_bytes=32 << 20),
        cost_estimate=pl.CostEstimate(
            flops=n_q * n_f * 8 * tokens * tokens * channels,
            transcendentals=n_q * n_f * 2 * tokens * tokens * heads,
            bytes_accessed=(n_f * 4 + n_q * 6) * tokens * channels * 2,
        ),
    )(*operands)
    outs = list(outs)
    return [outs.pop(0) if done else (outs.pop(0), outs.pop(0)) for done in finish]


def plan_four(pairs):
    def plan(z, first, second, i, f):
        query_set, frame = pairs[0][i], pairs[1][f]
        if (query_set, frame) in pairs[2]:
            return None
        middle = (z == 1) | (z == 2)
        ids = (z, 3 - z, 3 * (z - 1), 6 - 3 * z)
        mine = ids[0] if query_set == 0 else ids[2]
        times = (
            (ids[frame] == mine).astype(jnp.int32)
            + (first == ids[frame]).astype(jnp.int32)
            + (second == ids[frame]).astype(jnp.int32)
        )
        times = jnp.where(middle, times, 0)
        if (query_set, frame) in ((0, 1), (0, 2), (1, 0)):
            return times, middle & (ids[frame] == mine - 1)
        return times, None

    return plan


def plan_any(z, first, second, i, f):
    one = jnp.int32(1)
    if f == 1:
        return jnp.int32(0), z > 0
    return one, None


def four_frames(queries, keys, values, valid_prev, mem_index):
    shape = queries.shape
    width = shape[2]
    tokens = shape[1] * width

    def flat(block):
        return block.reshape(tokens, shape[3])

    query, key, value = flat(queries), flat(keys), flat(values)
    inward = [(0, 1), (3, 2)]
    across = [(1, 2), (2, 1)]
    end_key = moved(key, "frame", inward)
    end_value = moved(value, "frame", inward)
    mid_key = moved(key, "frame", across)
    mid_value = moved(value, "frame", across)
    marks = jnp.broadcast_to(valid_prev[0][:, None], (shape[1], shape[3])).astype(jnp.bfloat16)
    marks = jnp.pad(marks, ((0, 16 - shape[1]), (0, 0)))
    end_query = moved(jnp.concatenate([query, marks], 0), "frame", inward)
    far_key = moved(end_key, "frame", across)
    far_value = moved(end_value, "frame", across)
    end_valid = end_query[tokens : tokens + shape[1], 0].astype(jnp.int32)[None]
    end_query = end_query[:tokens]

    def frame(k, v):
        return [k, v, swapped(k), swapped(v)]

    own = frame(key, value)
    mid = frame(mid_key, mid_value)
    end = frame(end_key, end_value)
    far = frame(far_key, far_value)
    (state,) = attend(
        plan_four(((0,), (0,), ())), mem_index, [valid_prev], [query], [own], [None], [False], width
    )
    state, end_state = attend(
        plan_four(((0, 1), (0, 1, 2), ((0, 0),))),
        mem_index,
        [valid_prev, end_valid],
        [query, end_query],
        [own, mid, end],
        [state, None],
        [False, False],
        width,
    )
    (end_out,) = attend(
        plan_four(((1,), (3,), ())),
        mem_index,
        [end_valid],
        [end_query],
        [far],
        [end_state],
        [True],
        width,
    )
    back = moved(end_out, "frame", [(1, 0), (2, 3)])
    (out,) = attend(
        plan_four(((0,), (3,), ())), mem_index, [valid_prev], [query], [far], [state], [True], width
    )
    z = lax.axis_index("frame")
    return jnp.where((z == 1) | (z == 2), out, back).reshape(shape)


def any_frames(queries, keys, values, valid_prev, mem_index):
    shape = queries.shape
    width = shape[2]
    tokens = shape[1] * width
    count = lax.axis_size("frame")
    z = lax.axis_index("frame")

    def flat(block):
        return block.reshape(tokens, shape[3])

    query, key, value = flat(queries), flat(keys), flat(values)
    onward = [(i, i + 1) for i in range(count - 1)]
    prev = [moved(key, "frame", onward), moved(value, "frame", onward)]
    both = jnp.stack([key, value])
    masked = jnp.stack([jnp.where(z == mem_index[s], both, jnp.zeros_like(both)) for s in range(2)])
    memory = lax.psum(masked, "frame")
    frames = []
    for k, v in ((key, value), prev, memory[0], memory[1]):
        frames.append([k, v, swapped(k), swapped(v)])
    (out,) = attend(plan_any, mem_index, [valid_prev], [query], frames, [None], [True], width)
    return out.reshape(shape)


def solution(mesh):
    spread = P(("groups", "frame"), "row", None, "head")
    body = four_frames if mesh.shape["frame"] == 4 else any_frames
    return jax.shard_map(
        body,
        mesh=mesh,
        in_specs=(spread, spread, spread, P(("groups", "frame"), "row"), P("groups")),
        out_specs=spread,
        check_vma=False,
    )
```

time: 192 us -> 72.1 us (0.38)
  the two profiles are of different devices: /device:TPU:0 before, /device:TPU:27 now
where the time goes in v1:
time: 72.1 us; the launch traced here: 71.2 us
  waiting for transfers between devices  45.9 us (64%)
  starting transfers between devices  15.4 us (21%)
  Pallas kernels  5.78 us (8%)
  other arithmetic  2.02 us (3%)
  local copies, waits for them, and re-layouts  1.9 us (3%)
    ppermute x8, waiting for transfers between devices, moved(): return lax.ppermute(block, axis, pairs)  45.8 us
    ppermute x8, starting transfers between devices, moved(): return lax.ppermute(block, axis, pairs)  9.76 us
    pallas_call x4, Pallas kernels, attend(): pl.pallas_call(functools.partial(attend_kernel, plan, n_q, n_f, fresh, tu...  5.78 us
    ppermute x8, starting transfers between devices, swapped(): return lax.ppermute(block, 'row', [(0, 1), (1, 0)])  5.61 us
    unnamed x12, local copies, waits for them, and re-layouts  1.87 us
  transfers between devices with their start and end apart: 16, of which 3 were waited for; matrix products, arithmetic and copies ran while one was open for 2% of the time, Pallas kernels for 6%

profile of v1, /device:TPU:27, one launch (start us, length us, event | category | flops | bytes accessed | tf_op | source)
XLA Modules:
  0.0 71.2 jit_solution(8484051962579232725)
XLA Ops:
  0.0 0.7 collective-permute-start.7
  0.7 2.1 %collective-permute-start = (bf16[384,384]{1,0:T(8,128)(2,1)}, bf16[384,384]{1,0:T(8,128)(2,1)S(1)}, u32[]{:S(2)}, u32[]{:S(2)}) collective-permute-start(bf16[384,384]{1,0:T(8,128)(2,1)} %bitcast.14), channel_id=1, source_target_pairs={{0,4},{12,8},{1,5},{13,9},{2,6},{14,10},{3,7},{15,11},{16,20},{28,... | collective-permute-start | bytes 884744 | tf_op jit(solution)/shard_map/ppermute | solution.py:18
  2.8 0.5 collective-permute-start.8
  3.3 1.3 %collective-permute-start.2 = (bf16[384,384]{1,0:T(8,128)(2,1)}, bf16[384,384]{1,0:T(8,128)(2,1)S(1)}, u32[]{:S(2)}, u32[]{:S(2)}) collective-permute-start(bf16[384,384]{1,0:T(8,128)(2,1)} %bitcast.19), channel_id=1, source_target_pairs={{0,4},{12,8},{1,5},{13,9},{2,6},{14,10},{3,7},{15,11},{16,20},{28,... | collective-permute-start | bytes 884744 | tf_op jit(solution)/shard_map/ppermute | solution.py:18
  4.6 0.7 collective-permute-start.9
  5.3 0.0 copy-start
  5.3 0.0 copy-start.1
  5.3 0.0 copy-start.3
  5.3 1.1 %pad_maximum_fusion = bf16[400,384]{1,0:T(8,128)(2,1)S(1)} fusion(bf16[384,384]{1,0:T(8,128)(2,1)} %bitcast.7, bf16[400]{0:T(512)(128)(2,1)S(1)} %fusion), kind=kLoop, calls=%fused_computation | loop fusion | flops 614400 | bytes 602912 | tf_op jit(solution)/shard_map/concatenate | solution.py:207
  6.5 2.4 %collective-permute-start.6 = (bf16[400,384]{1,0:T(8,128)(2,1)S(1)}, bf16[400,384]{1,0:T(8,128)(2,1)S(1)}, u32[]{:S(2)}, u32[]{:S(2)}) collective-permute-start(bf16[400,384]{1,0:T(8,128)(2,1)S(1)} %pad_maximum_fusion), channel_id=1, source_target_pairs={{0,4},{12,8},{1,5},{13,9},{2,6},{14,10},{3,7},{15,11},{16,20},{28,... | collective-permute-start | bytes 921608 | tf_op jit(solution)/shard_map/ppermute | solution.py:18
  8.9 0.7 collective-permute-start.10
  9.6 1.2 %collective-permute-start.13 = (bf16[384,384]{1,0:T(8,128)(2,1)S(1)}, bf16[384,384]{1,0:T(8,128)(2,1)S(1)}, u32[]{:S(2)}, u32[]{:S(2)}) collective-permute-start(bf16[384,384]{1,0:T(8,128)(2,1)S(1)} %collective-permute-done.refs_13_), channel_id=1, source_target_pairs={{0,2},{2,0},{1,3},{3,1},{4,6},{6,4},{5,7},{7,5},{8,10},{10,8},{9,1... | collective-permute-start | bytes 884744 | tf_op jit(solution)/shard_map/ppermute | solution.py:22
  10.8 4.8 %collective-permute-done.2.refs_14_ = bf16[384,384]{1,0:T(8,128)(2,1)S(1)} collective-permute-done((bf16[384,384]{1,0:T(8,128)(2,1)}, bf16[384,384]{1,0:T(8,128)(2,1)S(1)}, u32[]{:S(2)}, u32[]{:S(2)}) %collective-permute-start.2) | collective-permute-done | bytes 294944 | tf_op jit(solution)/shard_map/ppermute | solution.py:18
  15.6 0.7 collective-permute-start.1
  16.3 0.7 collective-permute-start.3
  17.0 1.6 %collective-permute-start.14 = (bf16[384,384]{1,0:T(8,128)(2,1)S(1)}, bf16[384,384]{1,0:T(8,128)(2,1)S(1)}, u32[]{:S(2)}, u32[]{:S(2)}) collective-permute-start(bf16[384,384]{1,0:T(8,128)(2,1)S(1)} %collective-permute-done.2.refs_14_), channel_id=1, source_target_pairs={{0,2},{2,0},{1,3},{3,1},{4,6},{6,4},{5,7},{7,5},{8,10},{10,8},{9,1... | collective-permute-start | bytes 884744 | tf_op jit(solution)/shard_map/ppermute | solution.py:22
  18.6 3.5 %collective-permute-done.6 = bf16[400,384]{1,0:T(8,128)(2,1)S(1)} collective-permute-done((bf16[400,384]{1,0:T(8,128)(2,1)S(1)}, bf16[400,384]{1,0:T(8,128)(2,1)S(1)}, u32[]{:S(2)}, u32[]{:S(2)}) %collective-permute-start.6) | collective-permute-done | bytes 307232 | tf_op jit(solution)/shard_map/ppermute | solution.py:18
  22.1 1.0 %collective-permute-start.11 = (bf16[384,384]{1,0:T(8,128)(2,1)S(1)}, bf16[384,384]{1,0:T(8,128)(2,1)S(1)}, u32[]{:S(2)}, u32[]{:S(2)}) collective-permute-start(bf16[384,384]{1,0:T(8,128)(2,1)S(1)} %collective-permute-done.9.refs_9_), channel_id=1, source_target_pairs={{0,2},{2,0},{1,3},{3,1},{4,6},{6,4},{5,7},{7,5},{8,10},{10,8},{9,1... | collective-permute-start | bytes 884744 | tf_op jit(solution)/shard_map/ppermute | solution.py:22
  23.1 0.0 collective-permute-start.12
  23.1 0.0 copy-start.4
  23.1 1.0 %copy-done.4 = bf16[1,8,48,384]{3,2,1,0:T(8,128)(2,1)S(1)} copy-done((bf16[1,8,48,384]{3,2,1,0:T(8,128)(2,1)S(1)}, bf16[1,8,48,384]{3,2,1,0:T(8,128)(2,1)}, u32[]{:S(2)}) %copy-start.4) | copy-done | bytes 294936
  24.1 1.1 %shard_map.55 = (f32[384,384]{1,0:T(8,128)S(1)}, f32[384,384]{1,0:T(8,128)S(1)}) custom-call(s32[2]{0:T(128)S(1)} %copy-done.1, s32[1,8]{1,0:T(1,128)S(1)} %copy-done.2, bf16[384,384]{1,0:T(8,128)(2,1)S(1)} %bitcast.8, bf16[384,384]{1,0:T(8,128)(2,1)S(1)} %bitcast.16, bf16[384,384]{1,0:T(8,128)(2,1)S(1)} %bitcast.21, ...), custom_call_target="tpu_custom_call" | custom-call | flops 452984832 | bytes 2949120 | tf_op jit(solution)/shard_map/pallas_call | solution.py:141
  25.1 0.6 collective-permute-start.4
  25.7 0.1 collective-permute-start.5
  25.8 0.1 convert_reduce_fusion
  26.0 0.9 %copy-done.5 = bf16[1,8,48,384]{3,2,1,0:T(8,128)(2,1)S(1)} copy-done((bf16[1,8,48,384]{3,2,1,0:T(8,128)(2,1)S(1)}, bf16[1,8,48,384]{3,2,1,0:T(8,128)(2,1)}, u32[]{:S(2)}) %copy-start.5) | copy-done | bytes 294936
  26.9 2.0 %shard_map.56 = (f32[384,384]{1,0:T(8,128)S(1)}, f32[384,384]{1,0:T(8,128)S(1)}, f32[384,384]{1,0:T(8,128)S(1)}, f32[384,384]{1,0:T(8,128)S(1)}) custom-call(s32[2]{0:T(128)S(1)} %copy-done.1, s32[1,8]{1,0:T(1,128)S(1)} %copy-done.2, s32[1,8]{1,0:T(1,128)S(1)} %bitcast.11, bf16[384,384]{1,0:T(8,128)(2,1)S(1)} %bitcast.9, ...), custom_call_target="tpu_custom_call" | custom-call | flops 2717908992 | bytes 7077888 | tf_op jit(solution)/shard_map/pallas_call | solution.py:141
  28.9 1.4 %shard_map.58 = bf16[384,384]{1,0:T(8,128)(2,1)S(1)} custom-call(s32[2]{0:T(128)S(1)} %copy-done.1, s32[1,8]{1,0:T(1,128)S(1)} %bitcast.12, bf16[384,384]{1,0:T(8,128)(2,1)S(1)} %slice.9.refs_4_.refs_2_, bf16[384,384]{1,0:T(8,128)(2,1)S(1)} %collective-permute-done.1.refs_3_, bf16[384,384]{1,0:T(8,128)(2,1)S(1)} %collective-permute-done.3.refs_4_, ...), custom_call_target="tpu_custom_call" | custom-call | flops 452984832 | bytes 2949120 | tf_op jit(solution)/shard_map/pallas_call | solution.py:141
  30.3 1.3 %collective-permute-start.15 = (bf16[384,384]{1,0:T(8,128)(2,1)S(1)}, bf16[384,384]{1,0:T(8,128)(2,1)S(1)}, u32[]{:S(2)}, u32[]{:S(2)}) collective-permute-start(bf16[384,384]{1,0:T(8,128)(2,1)S(1)} %shard_map.58), channel_id=1, source_target_pairs={{4,0},{8,12},{5,1},{9,13},{6,2},{10,14},{7,3},{11,15},{20,16},{24,... | collective-permute-start | bytes 884744 | tf_op jit(solution)/shard_map/ppermute | solution.py:18
  31.6 1.4 %shard_map.57 = bf16[384,384]{1,0:T(8,128)(2,1)S(1)} custom-call(s32[2]{0:T(128)S(1)} %copy-done.1, s32[1,8]{1,0:T(1,128)S(1)} %copy-done.2, bf16[384,384]{1,0:T(8,128)(2,1)S(1)} %bitcast.10, bf16[384,384]{1,0:T(8,128)(2,1)S(1)} %collective-permute-done.1.refs_3_, bf16[384,384]{1,0:T(8,128)(2,1)S(1)} %collective-permute-done.3.refs_4_, ...), custom_call_target="tpu_custom_call" | custom-call | flops 452984832 | bytes 2949120 | tf_op jit(solution)/shard_map/pallas_call | solution.py:141
  32.9 37.5 %collective-permute-done.15 = bf16[384,384]{1,0:T(8,128)(2,1)S(1)} collective-permute-done((bf16[384,384]{1,0:T(8,128)(2,1)S(1)}, bf16[384,384]{1,0:T(8,128)(2,1)S(1)}, u32[]{:S(2)}, u32[]{:S(2)}) %collective-permute-start.15) | collective-permute-done | bytes 294944 | tf_op jit(solution)/shard_map/ppermute | solution.py:18
  70.5 0.8 %broadcast_select_fusion = bf16[384,384]{1,0:T(8,128)(2,1)} fusion(bf16[384,384]{1,0:T(8,128)(2,1)S(1)} %shard_map.57, bf16[384,384]{1,0:T(8,128)(2,1)S(1)} %collective-permute-done.15, pred[]{:T(512)S(6)} %or.3), kind=kLoop, calls=%fused_computation.1 | loop fusion | flops 147456 | bytes 884737 | tf_op jit(solution)/shard_map/jit(_where)/select_n | solution.py:248
  (22 shorter events, 0.1 us)
Async XLA Ops:
  0.0 5.3 %copy-start.2 = (s32[1,8]{1,0:T(1,128)S(1)}, s32[1,8]{1,0:T(1,128)}, u32[]{:S(2)}) copy-start(s32[1,8]{1,0:T(1,128)} %refs_1_.5) | copy-start | bytes 100
  0.0 6.5 %collective-permute-start.7 = (bf16[384,384]{1,0:T(8,128)(2,1)}, bf16[384,384]{1,0:T(8,128)(2,1)S(1)}, u32[]{:S(2)}, u32[]{:S(2)}) collective-permute-start(bf16[384,384]{1,0:T(8,128)(2,1)} %bitcast.13), channel_id=1, source_target_pairs={{0,2},{2,0},{1,3},{3,1},{4,6},{6,4},{5,7},{7,5},{8,10},{10,8},{9,1... | collective-permute-start | bytes 884744 | tf_op jit(solution)/shard_map/ppermute | solution.py:22
  0.7 8.9 %collective-permute-start = (bf16[384,384]{1,0:T(8,128)(2,1)}, bf16[384,384]{1,0:T(8,128)(2,1)S(1)}, u32[]{:S(2)}, u32[]{:S(2)}) collective-permute-start(bf16[384,384]{1,0:T(8,128)(2,1)} %bitcast.14), channel_id=1, source_target_pairs={{0,4},{12,8},{1,5},{13,9},{2,6},{14,10},{3,7},{15,11},{16,20},{28,... | collective-permute-start | bytes 884744 | tf_op jit(solution)/shard_map/ppermute | solution.py:18
  2.8 6.1 %collective-permute-start.8 = (bf16[384,384]{1,0:T(8,128)(2,1)}, bf16[384,384]{1,0:T(8,128)(2,1)S(1)}, u32[]{:S(2)}, u32[]{:S(2)}) collective-permute-start(bf16[384,384]{1,0:T(8,128)(2,1)} %bitcast.18), channel_id=1, source_target_pairs={{0,2},{2,0},{1,3},{3,1},{4,6},{6,4},{5,7},{7,5},{8,10},{10,8},{9,1... | collective-permute-start | bytes 884744 | tf_op jit(solution)/shard_map/ppermute | solution.py:22
  3.3 12.4 %collective-permute-start.2 = (bf16[384,384]{1,0:T(8,128)(2,1)}, bf16[384,384]{1,0:T(8,128)(2,1)S(1)}, u32[]{:S(2)}, u32[]{:S(2)}) collective-permute-start(bf16[384,384]{1,0:T(8,128)(2,1)} %bitcast.19), channel_id=1, source_target_pairs={{0,4},{12,8},{1,5},{13,9},{2,6},{14,10},{3,7},{15,11},{16,20},{28,... | collective-permute-start | bytes 884744 | tf_op jit(solution)/shard_map/ppermute | solution.py:18
  4.6 11.7 %collective-permute-start.9 = (bf16[384,384]{1,0:T(8,128)(2,1)}, bf16[384,384]{1,0:T(8,128)(2,1)S(1)}, u32[]{:S(2)}, u32[]{:S(2)}) collective-permute-start(bf16[384,384]{1,0:T(8,128)(2,1)} %bitcast.15), channel_id=1, source_target_pairs={{4,8},{8,4},{5,9},{9,5},{6,10},{10,6},{7,11},{11,7},{20,24},{24,20... | collective-permute-start | bytes 884744 | tf_op jit(solution)/shard_map/ppermute | solution.py:18
  5.3 17.8 %copy-start = (bf16[1,8,48,384]{3,2,1,0:T(8,128)(2,1)S(1)}, bf16[1,8,48,384]{3,2,1,0:T(8,128)(2,1)}, u32[]{:S(2)}) copy-start(bf16[1,8,48,384]{3,2,1,0:T(8,128)(2,1)} %param.5) | copy-start | bytes 884740
  5.3 17.8 %copy-start.1 = (s32[2]{0:T(128)S(1)}, s32[2]{0:T(128)}, u32[]{:S(2)}) copy-start(s32[2]{0:T(128)} %refs_0_.7) | copy-start | bytes 28
  5.3 17.8 %copy-start.3 = (bf16[1,8,48,384]{3,2,1,0:T(8,128)(2,1)S(1)}, bf16[1,8,48,384]{3,2,1,0:T(8,128)(2,1)}, u32[]{:S(2)}) copy-start(bf16[1,8,48,384]{3,2,1,0:T(8,128)(2,1)} %param.6) | copy-start | bytes 884740
  6.5 15.6 %collective-permute-start.6 = (bf16[400,384]{1,0:T(8,128)(2,1)S(1)}, bf16[400,384]{1,0:T(8,128)(2,1)S(1)}, u32[]{:S(2)}, u32[]{:S(2)}) collective-permute-start(bf16[400,384]{1,0:T(8,128)(2,1)S(1)} %pad_maximum_fusion), channel_id=1, source_target_pairs={{0,4},{12,8},{1,5},{13,9},{2,6},{14,10},{3,7},{15,11},{16,20},{28,... | collective-permute-start | bytes 921608 | tf_op jit(solution)/shard_map/ppermute | solution.py:18
  8.9 8.1 %collective-permute-start.10 = (bf16[384,384]{1,0:T(8,128)(2,1)}, bf16[384,384]{1,0:T(8,128)(2,1)S(1)}, u32[]{:S(2)}, u32[]{:S(2)}) collective-permute-start(bf16[384,384]{1,0:T(8,128)(2,1)} %bitcast.20), channel_id=1, source_target_pairs={{4,8},{8,4},{5,9},{9,5},{6,10},{10,6},{7,11},{11,7},{20,24},{24,20... | collective-permute-start | bytes 884744 | tf_op jit(solution)/shard_map/ppermute | solution.py:18
  9.6 13.5 %collective-permute-start.13 = (bf16[384,384]{1,0:T(8,128)(2,1)S(1)}, bf16[384,384]{1,0:T(8,128)(2,1)S(1)}, u32[]{:S(2)}, u32[]{:S(2)}) collective-permute-start(bf16[384,384]{1,0:T(8,128)(2,1)S(1)} %collective-permute-done.refs_13_), channel_id=1, source_target_pairs={{0,2},{2,0},{1,3},{3,1},{4,6},{6,4},{5,7},{7,5},{8,10},{10,8},{9,1... | collective-permute-start | bytes 884744 | tf_op jit(solution)/shard_map/ppermute | solution.py:22
  15.6 9.5 %collective-permute-start.1 = (bf16[384,384]{1,0:T(8,128)(2,1)S(1)}, bf16[384,384]{1,0:T(8,128)(2,1)S(1)}, u32[]{:S(2)}, u32[]{:S(2)}) collective-permute-start(bf16[384,384]{1,0:T(8,128)(2,1)S(1)} %collective-permute-done.refs_13_), channel_id=1, source_target_pairs={{4,8},{8,4},{5,9},{9,5},{6,10},{10,6},{7,11},{11,7},{20,24},{24,20... | collective-permute-start | bytes 884744 | tf_op jit(solution)/shard_map/ppermute | solution.py:18
  16.3 9.4 %collective-permute-start.3 = (bf16[384,384]{1,0:T(8,128)(2,1)S(1)}, bf16[384,384]{1,0:T(8,128)(2,1)S(1)}, u32[]{:S(2)}, u32[]{:S(2)}) collective-permute-start(bf16[384,384]{1,0:T(8,128)(2,1)S(1)} %collective-permute-done.2.refs_14_), channel_id=1, source_target_pairs={{4,8},{8,4},{5,9},{9,5},{6,10},{10,6},{7,11},{11,7},{20,24},{24,20... | collective-permute-start | bytes 884744 | tf_op jit(solution)/shard_map/ppermute | solution.py:18
  17.0 8.9 %collective-permute-start.14 = (bf16[384,384]{1,0:T(8,128)(2,1)S(1)}, bf16[384,384]{1,0:T(8,128)(2,1)S(1)}, u32[]{:S(2)}, u32[]{:S(2)}) collective-permute-start(bf16[384,384]{1,0:T(8,128)(2,1)S(1)} %collective-permute-done.2.refs_14_), channel_id=1, source_target_pairs={{0,2},{2,0},{1,3},{3,1},{4,6},{6,4},{5,7},{7,5},{8,10},{10,8},{9,1... | collective-permute-start | bytes 884744 | tf_op jit(solution)/shard_map/ppermute | solution.py:22
  22.1 3.8 %collective-permute-start.11 = (bf16[384,384]{1,0:T(8,128)(2,1)S(1)}, bf16[384,384]{1,0:T(8,128)(2,1)S(1)}, u32[]{:S(2)}, u32[]{:S(2)}) collective-permute-start(bf16[384,384]{1,0:T(8,128)(2,1)S(1)} %collective-permute-done.9.refs_9_), channel_id=1, source_target_pairs={{0,2},{2,0},{1,3},{3,1},{4,6},{6,4},{5,7},{7,5},{8,10},{10,8},{9,1... | collective-permute-start | bytes 884744 | tf_op jit(solution)/shard_map/ppermute | solution.py:22
  23.1 2.9 %collective-permute-start.12 = (bf16[384,384]{1,0:T(8,128)(2,1)S(1)}, bf16[384,384]{1,0:T(8,128)(2,1)S(1)}, u32[]{:S(2)}, u32[]{:S(2)}) collective-permute-start(bf16[384,384]{1,0:T(8,128)(2,1)S(1)} %collective-permute-done.10.refs_10_), channel_id=1, source_target_pairs={{0,2},{2,0},{1,3},{3,1},{4,6},{6,4},{5,7},{7,5},{8,10},{10,8},{9,1... | collective-permute-start | bytes 884744 | tf_op jit(solution)/shard_map/ppermute | solution.py:22
  23.1 1.0 %copy-start.4 = (bf16[1,8,48,384]{3,2,1,0:T(8,128)(2,1)S(1)}, bf16[1,8,48,384]{3,2,1,0:T(8,128)(2,1)}, u32[]{:S(2)}) copy-start(bf16[1,8,48,384]{3,2,1,0:T(8,128)(2,1)} %param.7) | copy-start | bytes 884740
  25.1 3.8 %collective-permute-start.4 = (bf16[384,384]{1,0:T(8,128)(2,1)S(1)}, bf16[384,384]{1,0:T(8,128)(2,1)S(1)}, u32[]{:S(2)}, u32[]{:S(2)}) collective-permute-start(bf16[384,384]{1,0:T(8,128)(2,1)S(1)} %collective-permute-done.1.refs_3_), channel_id=1, source_target_pairs={{0,2},{2,0},{1,3},{3,1},{4,6},{6,4},{5,7},{7,5},{8,10},{10,8},{9,1... | collective-permute-start | bytes 884744 | tf_op jit(solution)/shard_map/ppermute | solution.py:22
  25.7 3.2 %collective-permute-start.5 = (bf16[384,384]{1,0:T(8,128)(2,1)S(1)}, bf16[384,384]{1,0:T(8,128)(2,1)S(1)}, u32[]{:S(2)}, u32[]{:S(2)}) collective-permute-start(bf16[384,384]{1,0:T(8,128)(2,1)S(1)} %collective-permute-done.3.refs_4_), channel_id=1, source_target_pairs={{0,2},{2,0},{1,3},{3,1},{4,6},{6,4},{5,7},{7,5},{8,10},{10,8},{9,1... | collective-permute-start | bytes 884744 | tf_op jit(solution)/shard_map/ppermute | solution.py:22
  25.9 1.0 %copy-start.5 = (bf16[1,8,48,384]{3,2,1,0:T(8,128)(2,1)S(1)}, bf16[1,8,48,384]{3,2,1,0:T(8,128)(2,1)}, u32[]{:S(2)}) copy-start(bf16[1,8,48,384]{3,2,1,0:T(8,128)(2,1)} %param.7) | copy-start | bytes 884740
  30.3 40.2 %collective-permute-start.15 = (bf16[384,384]{1,0:T(8,128)(2,1)S(1)}, bf16[384,384]{1,0:T(8,128)(2,1)S(1)}, u32[]{:S(2)}, u32[]{:S(2)}) collective-permute-start(bf16[384,384]{1,0:T(8,128)(2,1)S(1)} %shard_map.58), channel_id=1, source_target_pairs={{4,0},{8,12},{5,1},{9,13},{6,2},{10,14},{7,3},{11,15},{20,16},{24,... | collective-permute-start | bytes 884744 | tf_op jit(solution)/shard_map/ppermute | solution.py:18

commit v2 on v1

v2 whole, which is shorter than its diff:
```python
import functools

import jax
import jax.numpy as jnp
from jax import lax
from jax.experimental import pallas as pl
from jax.experimental.pallas import tpu as pltpu
from jax.sharding import PartitionSpec as P

HEAD_DIM = 128
WINDOW = 2
SCALE = HEAD_DIM**-0.5 * 1.4426950408889634
FLOOR = -1e30
BLOCK = 128
LOG2_3 = 1.584962500721156


def moved(block, pairs):
    return lax.ppermute(block, "frame", pairs)


def swapped(block):
    return lax.ppermute(block, "row", [(0, 1), (1, 0)])


def log2_weight(count):
    return jnp.where(
        count < 1, -jnp.inf, jnp.where(count < 2, 0.0, jnp.where(count < 3, 1.0, LOG2_3))
    ).astype(jnp.float32)


def attend_kernel(plan, n_q, n_f, fresh, finish, windows, width, *refs):
    refs = list(refs)
    mem_ref = refs.pop(0)
    valid_refs = [refs.pop(0) for _ in range(n_q)]
    q_refs = [refs.pop(0) for _ in range(n_q)]
    frames = [[refs.pop(0) for _ in range(4)] for _ in range(n_f)]
    states = [None if fresh[i] else (refs.pop(0), refs.pop(0)) for i in range(n_q)]
    outs = [(refs.pop(0),) if finish[i] else (refs.pop(0), refs.pop(0)) for i in range(n_q)]
    query_buf, key_buf, value_buf, acc, peaks, sems = refs
    queries, channels = q_refs[0].shape
    heads = channels // HEAD_DIM
    rows = queries // width
    band = lax.axis_index("row")
    z = lax.axis_index("frame")

    copies = []
    for f in range(n_f):
        for half in range(2):
            for part, buf in enumerate((key_buf, value_buf)):
                copies.append(
                    pltpu.make_async_copy(
                        frames[f][2 * half + part],
                        buf.at[f, pl.ds(half * queries, queries), :],
                        sems.at[f, half, part],
                    )
                )
    for i in range(n_q):
        copies.append(pltpu.make_async_copy(q_refs[i], query_buf.at[i], sems.at[n_f + i, 0, 0]))
    for copy in copies:
        copy.start()

    for i in range(n_q):
        for h in range(heads):
            if fresh[i]:
                acc[i, h] = jnp.zeros(acc.shape[2:], jnp.float32)
                peaks[i, h] = jnp.full(peaks.shape[2:], FLOOR, jnp.float32)
            else:
                total, stat = states[i]
                acc[i, h, :, :HEAD_DIM] = total[:, pl.ds(h * HEAD_DIM, HEAD_DIM)]
                shape = (queries, HEAD_DIM)
                acc[i, h, :, HEAD_DIM:] = jnp.broadcast_to(
                    stat[:, heads + h : heads + h + 1], shape
                )
                peaks[i, h] = jnp.broadcast_to(stat[:, h : h + 1], shape)
    for copy in copies:
        copy.wait()

    ones = jnp.ones((2 * queries, HEAD_DIM), jnp.bfloat16)

    def step(i, f, times, window):
        factor = times.astype(jnp.float32)
        if window:
            outside, inside = log2_weight(times), log2_weight(times + 1)
            place = lax.broadcasted_iota(jnp.int32, (1, 2 * queries), 1)
            key_row = jnp.zeros((1, 2 * queries), jnp.int32)
            for r in range(1, 2 * rows):
                key_row = key_row + (place >= r * width).astype(jnp.int32)
            key_row = jnp.where(
                key_row < rows, key_row + band * rows, key_row - rows + (1 - band) * rows
            )
        for start in range(0, queries, BLOCK):
            part = pl.ds(start, BLOCK)
            if window:
                place = lax.broadcasted_iota(jnp.int32, (BLOCK, 1), 0) + start
                row = jnp.full((BLOCK, 1), -1000, jnp.int32)
                for r in range(rows):
                    valid = valid_refs[0][0, r]
                    if n_q > 1:
                        valid = jnp.where(i == 0, valid, valid_refs[1][0, r])
                    here = jnp.where(valid > 0, band * rows + r, -1000)
                    row = jnp.where((place >= r * width) & (place < (r + 1) * width), here, row)
                bias = jnp.where(jnp.abs(key_row - row) <= WINDOW, inside, outside)
            for h in range(heads):
                lanes = pl.ds(h * HEAD_DIM, HEAD_DIM)
                scores = (
                    lax.dot_general(
                        query_buf[i, part, lanes],
                        key_buf[f, :, lanes],
                        (((1,), (1,)), ((), ())),
                        preferred_element_type=jnp.float32,
                    )
                    * SCALE
                )
                if window:
                    scores = scores + bias
                old = peaks[i, h, part, :]
                peak = jnp.maximum(old, jnp.max(scores, axis=1, keepdims=True))
                terms = jnp.exp2(scores - peak[:, 0:1]).astype(jnp.bfloat16)
                value = jnp.concatenate([value_buf[f, :, lanes], ones], 1)
                mixed = jnp.dot(terms, value, preferred_element_type=jnp.float32)
                if not window:
                    mixed = mixed * factor
                fade = jnp.exp2(old - peak)
                acc[i, h, part, :] = (
                    acc[i, h, part, :] * jnp.concatenate([fade, fade], 1) + mixed
                )
                peaks[i, h, part, :] = peak

    def unit(u, carry):
        i, f = u // n_f, u % n_f
        times, window = plan(z, mem_ref[0], mem_ref[1], i, f)
        if windows:
            pl.when(window)(functools.partial(step, i, f, times, True))
            pl.when((times > 0) & jnp.logical_not(window))(
                functools.partial(step, i, f, times, False)
            )
        else:
            pl.when(times > 0)(functools.partial(step, i, f, times, False))
        return carry

    lax.fori_loop(0, n_q * n_f, unit, 0)

    for i in range(n_q):
        if finish[i]:
            for h in range(heads):
                outs[i][0][:, pl.ds(h * HEAD_DIM, HEAD_DIM)] = (
                    acc[i, h, :, :HEAD_DIM] / acc[i, h, :, HEAD_DIM:]
                ).astype(jnp.bfloat16)
        else:
            lane = lax.broadcasted_iota(jnp.int32, (1, HEAD_DIM), 1)
            stat = jnp.zeros((queries, HEAD_DIM), jnp.float32)
            for h in range(heads):
                outs[i][0][:, pl.ds(h * HEAD_DIM, HEAD_DIM)] = acc[i, h, :, :HEAD_DIM]
                stat = jnp.where(lane == h, peaks[i, h], stat)
                stat = jnp.where(lane == heads + h, acc[i, h, :, HEAD_DIM:], stat)
            outs[i][1][...] = stat


def attend(plan, windows, mem_index, valids, queries, frames, states, finish, width):
    n_q, n_f = len(queries), len(frames)
    tokens, channels = queries[0].shape
    heads = channels // HEAD_DIM
    scalars = pl.BlockSpec(memory_space=pltpu.SMEM)
    anywhere = pl.BlockSpec(memory_space=pltpu.HBM)
    whole = pl.BlockSpec(memory_space=pltpu.VMEM)
    fresh = tuple(s is None for s in states)
    operands = [mem_index, *valids, *queries]
    specs = [scalars] * (1 + n_q) + [anywhere] * n_q
    for frame in frames:
        operands += frame
        specs += [anywhere] * 4
    for state in states:
        if state is not None:
            operands += state
            specs += [whole] * 2
    shapes = []
    for done in finish:
        if done:
            shapes.append(jax.ShapeDtypeStruct((tokens, channels), jnp.bfloat16))
        else:
            shapes.append(jax.ShapeDtypeStruct((tokens, channels), jnp.float32))
            shapes.append(jax.ShapeDtypeStruct((tokens, HEAD_DIM), jnp.float32))
    outs = pl.pallas_call(
        functools.partial(
            attend_kernel, plan, n_q, n_f, fresh, tuple(finish), windows, width
        ),
        in_specs=specs,
        out_specs=[whole] * len(shapes),
        out_shape=shapes,
        scratch_shapes=[
            pltpu.VMEM((n_q, tokens, channels), jnp.bfloat16),
            pltpu.VMEM((n_f, 2 * tokens, channels), jnp.bfloat16),
            pltpu.VMEM((n_f, 2 * tokens, channels), jnp.bfloat16),
            pltpu.VMEM((n_q, heads, tokens, 2 * HEAD_DIM), jnp.float32),
            pltpu.VMEM((n_q, heads, tokens, HEAD_DIM), jnp.float32),
            pltpu.SemaphoreType.DMA((n_f + n_q, 2, 2)),
        ],
        compiler_params=pltpu.CompilerParams(vmem_limit_bytes=32 << 20),
        cost_estimate=pl.CostEstimate(
            flops=n_q * n_f * 8 * tokens * tokens * channels,
            transcendentals=n_q * n_f * 2 * tokens * tokens * heads,
            bytes_accessed=(n_f * 4 + n_q * 6) * tokens * channels * 2,
        ),
    )(*operands)
    outs = list(outs)
    return [outs.pop(0) if done else (outs.pop(0), outs.pop(0)) for done in finish]


def plan_four(sets, names, z, first, second, i, f):
    middle = (z == 1) | (z == 2)
    ids = (z, 3 - z, 3 * (z - 1), 6 - 3 * z)

    def pick(index, options):
        chosen = options[-1]
        for n in range(len(options) - 1):
            chosen = jnp.where(index == n, options[n], chosen)
        return chosen

    mine = pick(i, [(ids[0], ids[2])[s] for s in sets])
    frame = pick(f, [ids[n] for n in names])
    times = (
        (frame == mine).astype(jnp.int32)
        + (first == frame).astype(jnp.int32)
        + (second == frame).astype(jnp.int32)
    )
    return jnp.where(middle, times, 0), middle & (frame == mine - 1)


def plan_any(z, first, second, i, f):
    before = f == 1
    return jnp.where(before, 0, 1), before & (z > 0)


def with_other_half(key, value):
    return [key, value, swapped(key), swapped(value)]


def four_frames(queries, keys, values, valid_prev, mem_index):
    shape = queries.shape
    width = shape[2]
    tokens = shape[1] * width

    def flat(block):
        return block.reshape(tokens, shape[3])

    query, key, value = flat(queries), flat(keys), flat(values)
    inward = [(0, 1), (3, 2)]
    across = [(1, 2), (2, 1)]
    end_key, end_value = moved(key, inward), moved(value, inward)
    mid = with_other_half(moved(key, across), moved(value, across))
    own = with_other_half(key, value)
    end_key, end_value, late_query = lax.optimization_barrier((end_key, end_value, query))
    far_key, far_value = moved(end_key, across), moved(end_value, across)
    marks = jnp.broadcast_to(valid_prev[0][:, None], (shape[1], shape[3])).astype(jnp.bfloat16)
    marks = jnp.pad(marks, ((0, 16 - shape[1]), (0, 0)))
    end_query = moved(jnp.concatenate([late_query, marks], 0), inward)
    end_valid = end_query[tokens : tokens + shape[1], 0].astype(jnp.int32)[None]
    end_query = end_query[:tokens]
    end = with_other_half(end_key, end_value)
    (end_state,) = attend(
        functools.partial(plan_four, (1,), (0, 1, 2)),
        True,
        mem_index,
        [end_valid],
        [end_query],
        [own, mid, end],
        [None],
        [False],
        width,
    )
    far_key, far_value, end_state = lax.optimization_barrier((far_key, far_value, end_state))
    far = with_other_half(far_key, far_value)
    (end_out,) = attend(
        functools.partial(plan_four, (1,), (3,)),
        False,
        mem_index,
        [end_valid],
        [end_query],
        [far],
        [end_state],
        [True],
        width,
    )
    back = moved(end_out, [(1, 0), (2, 3)])
    (out,) = attend(
        functools.partial(plan_four, (0,), (0, 1, 2, 3)),
        True,
        mem_index,
        [valid_prev],
        [query],
        [own, mid, end, far],
        [None],
        [True],
        width,
    )
    z = lax.axis_index("frame")
    return jnp.where((z == 1) | (z == 2), out, back).reshape(shape)


def any_frames(queries, keys, values, valid_prev, mem_index):
    shape = queries.shape
    width = shape[2]
    tokens = shape[1] * width
    count = lax.axis_size("frame")
    z = lax.axis_index("frame")

    def flat(block):
        return block.reshape(tokens, shape[3])

    key, value = flat(keys), flat(values)
    onward = [(i, i + 1) for i in range(count - 1)]
    both = jnp.stack([key, value])
    masked = jnp.stack([jnp.where(z == mem_index[s], both, jnp.zeros_like(both)) for s in range(2)])
    memory = lax.psum(masked, "frame")
    frames = [
        with_other_half(key, value),
        with_other_half(moved(key, onward), moved(value, onward)),
        with_other_half(memory[0, 0], memory[0, 1]),
        with_other_half(memory[1, 0], memory[1, 1]),
    ]
    (out,) = attend(
        plan_any, True, mem_index, [valid_prev], [flat(queries)], frames, [None], [True], width
    )
    return out.reshape(shape)


def solution(mesh):
    spread = P(("groups", "frame"), "row", None, "head")
    body = four_frames if mesh.shape["frame"] == 4 else any_frames
    return jax.shard_map(
        body,
        mesh=mesh,
        in_specs=(spread, spread, spread, P(("groups", "frame"), "row"), P("groups")),
        out_specs=spread,
        check_vma=False,
    )
```

time: 72.1 us -> 60.7 us (0.84)
  the two profiles are of different devices: /device:TPU:27 before, /device:TPU:23 now
where the time goes in v2:
time: 60.7 us; the launch traced here: 60.5 us
  starting transfers between devices  24.5 us (40%)
  Pallas kernels  17 us (28%)
  waiting for transfers between devices  9.6 us (16%)
  local copies, waits for them, and re-layouts  7.11 us (12%)
  other arithmetic  1.98 us (3%)
    pallas_call x3, Pallas kernels, attend(): pl.pallas_call(functools.partial(attend_kernel, plan, n_q, n_f, fresh, tu...  17 us
    ppermute x8, starting transfers between devices, moved(): return lax.ppermute(block, 'frame', pairs)  15.6 us
    ppermute x8, starting transfers between devices, swapped(): return lax.ppermute(block, 'row', [(0, 1), (1, 0)])  8.96 us
    ppermute x8, waiting for transfers between devices, moved(): return lax.ppermute(block, 'frame', pairs)  7.44 us
    unnamed x34, local copies, waits for them, and re-layouts  7.08 us
    ppermute x8, waiting for transfers between devices, swapped(): return lax.ppermute(block, 'row', [(0, 1), (1, 0)])  2.16 us
  transfers between devices with their start and end apart: 16, of which 7 were waited for; matrix products, arithmetic and copies ran while one was open for 2% of the time, Pallas kernels for 23%

profile of v2, /device:TPU:23, one launch (start us, length us, event | category | flops | bytes accessed | tf_op | source)
XLA Modules:
  0.0 60.5 jit_solution(7703076668920458922)
XLA Ops:
  0.0 1.4 %collective-permute-start.6 = (bf16[384,384]{1,0:T(8,128)(2,1)}, bf16[384,384]{1,0:T(8,128)(2,1)S(1)}, u32[]{:S(2)}, u32[]{:S(2)}) collective-permute-start(bf16[384,384]{1,0:T(8,128)(2,1)} %bitcast.11), channel_id=1, source_target_pairs={{0,4},{12,8},{1,5},{13,9},{2,6},{14,10},{3,7},{15,11},{16,20},{28,... | collective-permute-start | bytes 884744 | tf_op jit(solution)/shard_map/ppermute | solution.py:19
  1.4 2.1 %collective-permute-start.2 = (bf16[384,384]{1,0:T(8,128)(2,1)}, bf16[384,384]{1,0:T(8,128)(2,1)S(1)}, u32[]{:S(2)}, u32[]{:S(2)}) collective-permute-start(bf16[384,384]{1,0:T(8,128)(2,1)} %bitcast.12), channel_id=1, source_target_pairs={{4,8},{8,4},{5,9},{9,5},{6,10},{10,6},{7,11},{11,7},{20,24},{24,20... | collective-permute-start | bytes 884744 | tf_op jit(solution)/shard_map/ppermute | solution.py:19
  3.5 1.3 %collective-permute-start.7 = (bf16[384,384]{1,0:T(8,128)(2,1)}, bf16[384,384]{1,0:T(8,128)(2,1)S(1)}, u32[]{:S(2)}, u32[]{:S(2)}) collective-permute-start(bf16[384,384]{1,0:T(8,128)(2,1)} %bitcast.16), channel_id=1, source_target_pairs={{0,4},{12,8},{1,5},{13,9},{2,6},{14,10},{3,7},{15,11},{16,20},{28,... | collective-permute-start | bytes 884744 | tf_op jit(solution)/shard_map/ppermute | solution.py:19
  4.8 3.2 %collective-permute-start.3 = (bf16[384,384]{1,0:T(8,128)(2,1)}, bf16[384,384]{1,0:T(8,128)(2,1)S(1)}, u32[]{:S(2)}, u32[]{:S(2)}) collective-permute-start(bf16[384,384]{1,0:T(8,128)(2,1)} %bitcast.17), channel_id=1, source_target_pairs={{4,8},{8,4},{5,9},{9,5},{6,10},{10,6},{7,11},{11,7},{20,24},{24,20... | collective-permute-start | bytes 884744 | tf_op jit(solution)/shard_map/ppermute | solution.py:19
  8.0 1.3 %collective-permute-start = (bf16[384,384]{1,0:T(8,128)(2,1)}, bf16[384,384]{1,0:T(8,128)(2,1)S(1)}, u32[]{:S(2)}, u32[]{:S(2)}) collective-permute-start(bf16[384,384]{1,0:T(8,128)(2,1)} %bitcast.13), channel_id=1, source_target_pairs={{0,2},{2,0},{1,3},{3,1},{4,6},{6,4},{5,7},{7,5},{8,10},{10,8},{9,1... | collective-permute-start | bytes 884744 | tf_op jit(solution)/shard_map/ppermute | solution.py:23
  9.3 0.8 %collective-permute-done.6.refs_11_ = bf16[384,384]{1,0:T(8,128)(2,1)S(1)} collective-permute-done((bf16[384,384]{1,0:T(8,128)(2,1)}, bf16[384,384]{1,0:T(8,128)(2,1)S(1)}, u32[]{:S(2)}, u32[]{:S(2)}) %collective-permute-start.6) | collective-permute-done | bytes 294944 | tf_op jit(solution)/shard_map/ppermute | solution.py:19
  10.1 2.7 %collective-permute-start.1 = (bf16[384,384]{1,0:T(8,128)(2,1)}, bf16[384,384]{1,0:T(8,128)(2,1)S(1)}, u32[]{:S(2)}, u32[]{:S(2)}) collective-permute-start(bf16[384,384]{1,0:T(8,128)(2,1)} %bitcast.18), channel_id=1, source_target_pairs={{0,2},{2,0},{1,3},{3,1},{4,6},{6,4},{5,7},{7,5},{8,10},{10,8},{9,1... | collective-permute-start | bytes 884744 | tf_op jit(solution)/shard_map/ppermute | solution.py:23
  12.8 3.6 %collective-permute-done.7.refs_12_ = bf16[384,384]{1,0:T(8,128)(2,1)S(1)} collective-permute-done((bf16[384,384]{1,0:T(8,128)(2,1)}, bf16[384,384]{1,0:T(8,128)(2,1)S(1)}, u32[]{:S(2)}, u32[]{:S(2)}) %collective-permute-start.7) | collective-permute-done | bytes 294944 | tf_op jit(solution)/shard_map/ppermute | solution.py:19
  16.4 1.1 %pad_maximum_fusion = bf16[400,384]{1,0:T(8,128)(2,1)S(1)} fusion(bf16[384,384]{1,0:T(8,128)(2,1)} %bitcast.7, bf16[400]{0:T(512)(128)(2,1)S(1)} %fusion), kind=kLoop, calls=%fused_computation | loop fusion | flops 614400 | bytes 602912 | tf_op jit(solution)/shard_map/concatenate | solution.py:257
  17.5 1.4 %collective-permute-start.12 = (bf16[400,384]{1,0:T(8,128)(2,1)S(1)}, bf16[400,384]{1,0:T(8,128)(2,1)S(1)}, u32[]{:S(2)}, u32[]{:S(2)}) collective-permute-start(bf16[400,384]{1,0:T(8,128)(2,1)S(1)} %pad_maximum_fusion), channel_id=1, source_target_pairs={{0,4},{12,8},{1,5},{13,9},{2,6},{14,10},{3,7},{15,11},{16,20},{28,... | collective-permute-start | bytes 921608 | tf_op jit(solution)/shard_map/ppermute | solution.py:19
  19.0 1.6 %collective-permute-start.8 = (bf16[384,384]{1,0:T(8,128)(2,1)S(1)}, bf16[384,384]{1,0:T(8,128)(2,1)S(1)}, u32[]{:S(2)}, u32[]{:S(2)}) collective-permute-start(bf16[384,384]{1,0:T(8,128)(2,1)S(1)} %collective-permute-done.6.refs_11_), channel_id=1, source_target_pairs={{0,2},{2,0},{1,3},{3,1},{4,6},{6,4},{5,7},{7,5},{8,10},{10,8},{9,1... | collective-permute-start | bytes 884744 | tf_op jit(solution)/shard_map/ppermute | solution.py:23
  20.7 0.4 collective-permute-start.4
  21.2 0.6 collective-permute-done.8.refs_13_
  21.8 2.1 %collective-permute-start.10 = (bf16[384,384]{1,0:T(8,128)(2,1)S(1)}, bf16[384,384]{1,0:T(8,128)(2,1)S(1)}, u32[]{:S(2)}, u32[]{:S(2)}) collective-permute-start(bf16[384,384]{1,0:T(8,128)(2,1)S(1)} %collective-permute-done.6.refs_11_), channel_id=1, source_target_pairs={{4,8},{8,4},{5,9},{9,5},{6,10},{10,6},{7,11},{11,7},{20,24},{24,20... | collective-permute-start | bytes 884744 | tf_op jit(solution)/shard_map/ppermute | solution.py:19
  23.9 2.9 %collective-permute-done.12 = bf16[400,384]{1,0:T(8,128)(2,1)S(1)} collective-permute-done((bf16[400,384]{1,0:T(8,128)(2,1)S(1)}, bf16[400,384]{1,0:T(8,128)(2,1)S(1)}, u32[]{:S(2)}, u32[]{:S(2)}) %collective-permute-start.12) | collective-permute-done | bytes 307232 | tf_op jit(solution)/shard_map/ppermute | solution.py:19
  26.8 2.1 %collective-permute-start.11 = (bf16[384,384]{1,0:T(8,128)(2,1)S(1)}, bf16[384,384]{1,0:T(8,128)(2,1)S(1)}, u32[]{:S(2)}, u32[]{:S(2)}) collective-permute-start(bf16[384,384]{1,0:T(8,128)(2,1)S(1)} %collective-permute-done.7.refs_12_), channel_id=1, source_target_pairs={{4,8},{8,4},{5,9},{9,5},{6,10},{10,6},{7,11},{11,7},{20,24},{24,20... | collective-permute-start | bytes 884744 | tf_op jit(solution)/shard_map/ppermute | solution.py:19
  29.1 0.6 copy-done.1
  29.7 6.8 %shard_map.55 = (f32[384,384]{1,0:T(8,128)S(1)}, f32[384,128]{1,0:T(8,128)S(1)}) custom-call(s32[2]{0:T(128)S(1)} %copy-done.1, s32[1,8]{1,0:T(1,128)S(1)} %bitcast.9, bf16[384,384]{1,0:T(8,128)(2,1)S(1)} %slice.9.refs_2_, bf16[384,384]{1,0:T(8,128)(2,1)S(1)} %bitcast.14, bf16[384,384]{1,0:T(8,128)(2,1)S(1)} %bitcast.19, ...), custom_call_target="tpu_custom_call" | custom-call | flops 1358954496 | bytes 5308416 | tf_op jit(solution)/shard_map/pallas_call | solution.py:184
  36.5 0.7 %copy-done.8 = bf16[384,384]{1,0:T(8,128)(2,1)} copy-done((bf16[384,384]{1,0:T(8,128)(2,1)}, bf16[384,384]{1,0:T(8,128)(2,1)S(1)}, u32[]{:S(2)}) %copy-start.8) | copy-done | bytes 294936
  37.4 2.7 %collective-permute-start.13 = (bf16[384,384]{1,0:T(8,128)(2,1)S(1)}, bf16[384,384]{1,0:T(8,128)(2,1)S(1)}, u32[]{:S(2)}, u32[]{:S(2)}) collective-permute-start(bf16[384,384]{1,0:T(8,128)(2,1)S(1)} %collective-permute-done.10.refs_15_.refs_3_), channel_id=1, source_target_pairs={{0,2},{2,0},{1,3},{3,1},{4,6},{6,4},{5,7},{7,5},{8,10},{10,8},{9,1... | collective-permute-start | bytes 884744 | tf_op jit(solution)/shard_map/ppermute | solution.py:23
  40.1 1.1 %collective-permute-done.13.refs_17_.refs_5_ = bf16[384,384]{1,0:T(8,128)(2,1)S(1)} collective-permute-done((bf16[384,384]{1,0:T(8,128)(2,1)S(1)}, bf16[384,384]{1,0:T(8,128)(2,1)S(1)}, u32[]{:S(2)}, u32[]{:S(2)}) %collective-permute-start.13) | collective-permute-done | bytes 294944 | tf_op jit(solution)/shard_map/ppermute | solution.py:23
  41.3 0.4 collective-permute-done.14.refs_18_.refs_6_
  41.7 3.1 %shard_map.57 = bf16[384,384]{1,0:T(8,128)(2,1)S(1)} custom-call(s32[2]{0:T(128)S(1)} %copy-done.1, s32[1,8]{1,0:T(1,128)S(1)} %bitcast.10, bf16[384,384]{1,0:T(8,128)(2,1)S(1)} %slice.9.refs_2_, bf16[384,384]{1,0:T(8,128)(2,1)S(1)} %collective-permute-done.10.refs_15_.refs_3_, bf16[384,384]{1,0:T(8,128)(2,1)S(1)} %collective-permute-done.11.refs_16_.refs_4_, ...), custom_call_target="tpu_custom_call" | custom-call | flops 452984832 | bytes 2949120 | tf_op jit(solution)/shard_map/pallas_call | solution.py:184
  44.8 2.0 %collective-permute-start.15 = (bf16[384,384]{1,0:T(8,128)(2,1)S(1)}, bf16[384,384]{1,0:T(8,128)(2,1)}, u32[]{:S(2)}, u32[]{:S(2)}) collective-permute-start(bf16[384,384]{1,0:T(8,128)(2,1)S(1)} %shard_map.57), channel_id=1, source_target_pairs={{4,0},{8,12},{5,1},{9,13},{6,2},{10,14},{7,3},{11,15},{20,16},{24,... | collective-permute-start | bytes 884744 | tf_op jit(solution)/shard_map/ppermute | solution.py:19
  46.8 1.0 %copy-done.5 = bf16[384,384]{1,0:T(8,128)(2,1)S(1)} copy-done((bf16[384,384]{1,0:T(8,128)(2,1)S(1)}, bf16[384,384]{1,0:T(8,128)(2,1)}, u32[]{:S(2)}) %copy-start.5) | copy-done | bytes 294936
  47.7 1.0 %copy-done.7 = bf16[384,384]{1,0:T(8,128)(2,1)S(1)} copy-done((bf16[384,384]{1,0:T(8,128)(2,1)S(1)}, bf16[384,384]{1,0:T(8,128)(2,1)}, u32[]{:S(2)}) %copy-start.7) | copy-done | bytes 294936
  48.7 1.0 %copy-done.9 = bf16[384,384]{1,0:T(8,128)(2,1)S(1)} copy-done((bf16[384,384]{1,0:T(8,128)(2,1)S(1)}, bf16[384,384]{1,0:T(8,128)(2,1)}, u32[]{:S(2)}) %copy-start.9) | copy-done | bytes 294936
  49.7 1.0 %copy-done.11 = bf16[384,384]{1,0:T(8,128)(2,1)S(1)} copy-done((bf16[384,384]{1,0:T(8,128)(2,1)S(1)}, bf16[384,384]{1,0:T(8,128)(2,1)}, u32[]{:S(2)}) %copy-start.11) | copy-done | bytes 294936
  50.6 1.0 %copy-done.13 = bf16[384,384]{1,0:T(8,128)(2,1)S(1)} copy-done((bf16[384,384]{1,0:T(8,128)(2,1)S(1)}, bf16[384,384]{1,0:T(8,128)(2,1)}, u32[]{:S(2)}) %copy-start.13) | copy-done | bytes 294936
  51.6 1.0 %copy-done.15 = bf16[384,384]{1,0:T(8,128)(2,1)S(1)} copy-done((bf16[384,384]{1,0:T(8,128)(2,1)S(1)}, bf16[384,384]{1,0:T(8,128)(2,1)}, u32[]{:S(2)}) %copy-start.15) | copy-done | bytes 294936
  52.6 7.1 %shard_map.56 = bf16[384,384]{1,0:T(8,128)(2,1)S(1)} custom-call(s32[2]{0:T(128)S(1)} %copy-done.1, s32[1,8]{1,0:T(1,128)S(1)} %copy-done.16, bf16[384,384]{1,0:T(8,128)(2,1)S(1)} %bitcast.8, bf16[384,384]{1,0:T(8,128)(2,1)S(1)} %bitcast.15, bf16[384,384]{1,0:T(8,128)(2,1)S(1)} %bitcast.20, bf16[384,384]{1,0:T(8,128)(2,1)S(1)} %copy-done.5, ...), custom_call_target="tpu_custom_call" | custom-call | flops 1811939328 | bytes 6488064 | tf_op jit(solution)/shard_map/pallas_call | solution.py:184
  59.7 0.8 %broadcast_select_fusion = bf16[384,384]{1,0:T(8,128)(2,1)} fusion(bf16[384,384]{1,0:T(8,128)(2,1)S(1)} %shard_map.56, bf16[384,384]{1,0:T(8,128)(2,1)} %collective-permute-done.15, pred[]{:T(512)S(6)} %or.3), kind=kLoop, calls=%fused_computation.1 | loop fusion | flops 147456 | bytes 884737 | tf_op jit(solution)/shard_map/jit(_where)/select_n | solution.py:298
  (43 shorter events, 0.6 us)
Async XLA Ops:
  0.0 9.3 %copy-start.16 = (s32[1,8]{1,0:T(1,128)S(1)}, s32[1,8]{1,0:T(1,128)}, u32[]{:S(2)}) copy-start(s32[1,8]{1,0:T(1,128)} %refs_1_.1) | copy-start | bytes 100
  0.0 10.1 %collective-permute-start.6 = (bf16[384,384]{1,0:T(8,128)(2,1)}, bf16[384,384]{1,0:T(8,128)(2,1)S(1)}, u32[]{:S(2)}, u32[]{:S(2)}) collective-permute-start(bf16[384,384]{1,0:T(8,128)(2,1)} %bitcast.11), channel_id=1, source_target_pairs={{0,4},{12,8},{1,5},{13,9},{2,6},{14,10},{3,7},{15,11},{16,20},{28,... | collective-permute-start | bytes 884744 | tf_op jit(solution)/shard_map/ppermute | solution.py:19
  1.4 17.5 %collective-permute-start.2 = (bf16[384,384]{1,0:T(8,128)(2,1)}, bf16[384,384]{1,0:T(8,128)(2,1)S(1)}, u32[]{:S(2)}, u32[]{:S(2)}) collective-permute-start(bf16[384,384]{1,0:T(8,128)(2,1)} %bitcast.12), channel_id=1, source_target_pairs={{4,8},{8,4},{5,9},{9,5},{6,10},{10,6},{7,11},{11,7},{20,24},{24,20... | collective-permute-start | bytes 884744 | tf_op jit(solution)/shard_map/ppermute | solution.py:19
  3.5 12.9 %collective-permute-start.7 = (bf16[384,384]{1,0:T(8,128)(2,1)}, bf16[384,384]{1,0:T(8,128)(2,1)S(1)}, u32[]{:S(2)}, u32[]{:S(2)}) collective-permute-start(bf16[384,384]{1,0:T(8,128)(2,1)} %bitcast.16), channel_id=1, source_target_pairs={{0,4},{12,8},{1,5},{13,9},{2,6},{14,10},{3,7},{15,11},{16,20},{28,... | collective-permute-start | bytes 884744 | tf_op jit(solution)/shard_map/ppermute | solution.py:19
  4.8 15.8 %collective-permute-start.3 = (bf16[384,384]{1,0:T(8,128)(2,1)}, bf16[384,384]{1,0:T(8,128)(2,1)S(1)}, u32[]{:S(2)}, u32[]{:S(2)}) collective-permute-start(bf16[384,384]{1,0:T(8,128)(2,1)} %bitcast.17), channel_id=1, source_target_pairs={{4,8},{8,4},{5,9},{9,5},{6,10},{10,6},{7,11},{11,7},{20,24},{24,20... | collective-permute-start | bytes 884744 | tf_op jit(solution)/shard_map/ppermute | solution.py:19
  8.0 12.7 %collective-permute-start = (bf16[384,384]{1,0:T(8,128)(2,1)}, bf16[384,384]{1,0:T(8,128)(2,1)S(1)}, u32[]{:S(2)}, u32[]{:S(2)}) collective-permute-start(bf16[384,384]{1,0:T(8,128)(2,1)} %bitcast.13), channel_id=1, source_target_pairs={{0,2},{2,0},{1,3},{3,1},{4,6},{6,4},{5,7},{7,5},{8,10},{10,8},{9,1... | collective-permute-start | bytes 884744 | tf_op jit(solution)/shard_map/ppermute | solution.py:23
  10.1 11.0 %collective-permute-start.1 = (bf16[384,384]{1,0:T(8,128)(2,1)}, bf16[384,384]{1,0:T(8,128)(2,1)S(1)}, u32[]{:S(2)}, u32[]{:S(2)}) collective-permute-start(bf16[384,384]{1,0:T(8,128)(2,1)} %bitcast.18), channel_id=1, source_target_pairs={{0,2},{2,0},{1,3},{3,1},{4,6},{6,4},{5,7},{7,5},{8,10},{10,8},{9,1... | collective-permute-start | bytes 884744 | tf_op jit(solution)/shard_map/ppermute | solution.py:23
  17.5 11.6 %copy-start.2 = (bf16[1,8,48,384]{3,2,1,0:T(8,128)(2,1)S(1)}, bf16[1,8,48,384]{3,2,1,0:T(8,128)(2,1)}, u32[]{:S(2)}) copy-start(bf16[1,8,48,384]{3,2,1,0:T(8,128)(2,1)} %param.6) | copy-start | bytes 884740
  17.5 11.6 %copy-start.3 = (bf16[1,8,48,384]{3,2,1,0:T(8,128)(2,1)S(1)}, bf16[1,8,48,384]{3,2,1,0:T(8,128)(2,1)}, u32[]{:S(2)}) copy-start(bf16[1,8,48,384]{3,2,1,0:T(8,128)(2,1)} %param.7) | copy-start | bytes 884740
  17.5 9.2 %collective-permute-start.12 = (bf16[400,384]{1,0:T(8,128)(2,1)S(1)}, bf16[400,384]{1,0:T(8,128)(2,1)S(1)}, u32[]{:S(2)}, u32[]{:S(2)}) collective-permute-start(bf16[400,384]{1,0:T(8,128)(2,1)S(1)} %pad_maximum_fusion), channel_id=1, source_target_pairs={{0,4},{12,8},{1,5},{13,9},{2,6},{14,10},{3,7},{15,11},{16,20},{28,... | collective-permute-start | bytes 921608 | tf_op jit(solution)/shard_map/ppermute | solution.py:19
  19.0 2.8 %collective-permute-start.8 = (bf16[384,384]{1,0:T(8,128)(2,1)S(1)}, bf16[384,384]{1,0:T(8,128)(2,1)S(1)}, u32[]{:S(2)}, u32[]{:S(2)}) collective-permute-start(bf16[384,384]{1,0:T(8,128)(2,1)S(1)} %collective-permute-done.6.refs_11_), channel_id=1, source_target_pairs={{0,2},{2,0},{1,3},{3,1},{4,6},{6,4},{5,7},{7,5},{8,10},{10,8},{9,1... | collective-permute-start | bytes 884744 | tf_op jit(solution)/shard_map/ppermute | solution.py:23
  20.6 8.4 %collective-permute-start.9 = (bf16[384,384]{1,0:T(8,128)(2,1)S(1)}, bf16[384,384]{1,0:T(8,128)(2,1)S(1)}, u32[]{:S(2)}, u32[]{:S(2)}) collective-permute-start(bf16[384,384]{1,0:T(8,128)(2,1)S(1)} %collective-permute-done.7.refs_12_), channel_id=1, source_target_pairs={{0,2},{2,0},{1,3},{3,1},{4,6},{6,4},{5,7},{7,5},{8,10},{10,8},{9,1... | collective-permute-start | bytes 884744 | tf_op jit(solution)/shard_map/ppermute | solution.py:23
  20.7 8.4 %copy-start.4 = (bf16[384,384]{1,0:T(8,128)(2,1)}, bf16[384,384]{1,0:T(8,128)(2,1)S(1)}, u32[]{:S(2)}) copy-start(bf16[384,384]{1,0:T(8,128)(2,1)S(1)} %collective-permute-done.refs_5_) | copy-start | bytes 884740
  20.7 8.4 %collective-permute-start.4 = (bf16[384,384]{1,0:T(8,128)(2,1)S(1)}, bf16[384,384]{1,0:T(8,128)(2,1)S(1)}, u32[]{:S(2)}, u32[]{:S(2)}) collective-permute-start(bf16[384,384]{1,0:T(8,128)(2,1)S(1)} %collective-permute-done.2.refs_7_), channel_id=1, source_target_pairs={{0,2},{2,0},{1,3},{3,1},{4,6},{6,4},{5,7},{7,5},{8,10},{10,8},{9,1... | collective-permute-start | bytes 884744 | tf_op jit(solution)/shard_map/ppermute | solution.py:23
  21.1 8.0 %copy-start.6 = (bf16[384,384]{1,0:T(8,128)(2,1)}, bf16[384,384]{1,0:T(8,128)(2,1)S(1)}, u32[]{:S(2)}) copy-start(bf16[384,384]{1,0:T(8,128)(2,1)S(1)} %collective-permute-done.1.refs_6_) | copy-start | bytes 884740
  21.1 7.9 %collective-permute-start.5 = (bf16[384,384]{1,0:T(8,128)(2,1)S(1)}, bf16[384,384]{1,0:T(8,128)(2,1)S(1)}, u32[]{:S(2)}, u32[]{:S(2)}) collective-permute-start(bf16[384,384]{1,0:T(8,128)(2,1)S(1)} %collective-permute-done.3.refs_8_), channel_id=1, source_target_pairs={{0,2},{2,0},{1,3},{3,1},{4,6},{6,4},{5,7},{7,5},{8,10},{10,8},{9,1... | collective-permute-start | bytes 884744 | tf_op jit(solution)/shard_map/ppermute | solution.py:23
  21.8 15.4 %collective-permute-start.10 = (bf16[384,384]{1,0:T(8,128)(2,1)S(1)}, bf16[384,384]{1,0:T(8,128)(2,1)S(1)}, u32[]{:S(2)}, u32[]{:S(2)}) collective-permute-start(bf16[384,384]{1,0:T(8,128)(2,1)S(1)} %collective-permute-done.6.refs_11_), channel_id=1, source_target_pairs={{4,8},{8,4},{5,9},{9,5},{6,10},{10,6},{7,11},{11,7},{20,24},{24,20... | collective-permute-start | bytes 884744 | tf_op jit(solution)/shard_map/ppermute | solution.py:19
  26.8 10.6 %collective-permute-start.11 = (bf16[384,384]{1,0:T(8,128)(2,1)S(1)}, bf16[384,384]{1,0:T(8,128)(2,1)S(1)}, u32[]{:S(2)}, u32[]{:S(2)}) collective-permute-start(bf16[384,384]{1,0:T(8,128)(2,1)S(1)} %collective-permute-done.7.refs_12_), channel_id=1, source_target_pairs={{4,8},{8,4},{5,9},{9,5},{6,10},{10,6},{7,11},{11,7},{20,24},{24,20... | collective-permute-start | bytes 884744 | tf_op jit(solution)/shard_map/ppermute | solution.py:19
  29.0 7.5 %copy-start.10 = (bf16[384,384]{1,0:T(8,128)(2,1)}, bf16[384,384]{1,0:T(8,128)(2,1)S(1)}, u32[]{:S(2)}) copy-start(bf16[384,384]{1,0:T(8,128)(2,1)S(1)} %collective-permute-done.9.refs_14_) | copy-start | bytes 884740
  29.0 7.4 %copy-start.12 = (bf16[384,384]{1,0:T(8,128)(2,1)}, bf16[384,384]{1,0:T(8,128)(2,1)S(1)}, u32[]{:S(2)}) copy-start(bf16[384,384]{1,0:T(8,128)(2,1)S(1)} %collective-permute-done.4.refs_9_) | copy-start | bytes 884740
  29.1 7.4 %copy-start.14 = (bf16[384,384]{1,0:T(8,128)(2,1)}, bf16[384,384]{1,0:T(8,128)(2,1)S(1)}, u32[]{:S(2)}) copy-start(bf16[384,384]{1,0:T(8,128)(2,1)S(1)} %collective-permute-done.5.refs_10_) | copy-start | bytes 884740
  36.5 0.7 %copy-start.8 = (bf16[384,384]{1,0:T(8,128)(2,1)}, bf16[384,384]{1,0:T(8,128)(2,1)S(1)}, u32[]{:S(2)}) copy-start(bf16[384,384]{1,0:T(8,128)(2,1)S(1)} %collective-permute-done.8.refs_13_) | copy-start | bytes 884740
  37.4 9.4 %copy-start = (bf16[1,8,48,384]{3,2,1,0:T(8,128)(2,1)S(1)}, bf16[1,8,48,384]{3,2,1,0:T(8,128)(2,1)}, u32[]{:S(2)}) copy-start(bf16[1,8,48,384]{3,2,1,0:T(8,128)(2,1)} %param.5) | copy-start | bytes 884740
  37.4 3.9 %collective-permute-start.13 = (bf16[384,384]{1,0:T(8,128)(2,1)S(1)}, bf16[384,384]{1,0:T(8,128)(2,1)S(1)}, u32[]{:S(2)}, u32[]{:S(2)}) collective-permute-start(bf16[384,384]{1,0:T(8,128)(2,1)S(1)} %collective-permute-done.10.refs_15_.refs_3_), channel_id=1, source_target_pairs={{0,2},{2,0},{1,3},{3,1},{4,6},{6,4},{5,7},{7,5},{8,10},{10,8},{9,1... | collective-permute-start | bytes 884744 | tf_op jit(solution)/shard_map/ppermute | solution.py:23
  40.1 1.6 %collective-permute-start.14 = (bf16[384,384]{1,0:T(8,128)(2,1)S(1)}, bf16[384,384]{1,0:T(8,128)(2,1)S(1)}, u32[]{:S(2)}, u32[]{:S(2)}) collective-permute-start(bf16[384,384]{1,0:T(8,128)(2,1)S(1)} %collective-permute-done.11.refs_16_.refs_4_), channel_id=1, source_target_pairs={{0,2},{2,0},{1,3},{3,1},{4,6},{6,4},{5,7},{7,5},{8,10},{10,8},{9,1... | collective-permute-start | bytes 884744 | tf_op jit(solution)/shard_map/ppermute | solution.py:23
  44.8 14.9 %collective-permute-start.15 = (bf16[384,384]{1,0:T(8,128)(2,1)S(1)}, bf16[384,384]{1,0:T(8,128)(2,1)}, u32[]{:S(2)}, u32[]{:S(2)}) collective-permute-start(bf16[384,384]{1,0:T(8,128)(2,1)S(1)} %shard_map.57), channel_id=1, source_target_pairs={{4,0},{8,12},{5,1},{9,13},{6,2},{10,14},{7,3},{11,15},{20,16},{24,... | collective-permute-start | bytes 884744 | tf_op jit(solution)/shard_map/ppermute | solution.py:19
  46.8 1.0 %copy-start.5 = (bf16[384,384]{1,0:T(8,128)(2,1)S(1)}, bf16[384,384]{1,0:T(8,128)(2,1)}, u32[]{:S(2)}) copy-start(bf16[384,384]{1,0:T(8,128)(2,1)} %copy-done.4) | copy-start | bytes 884740
  47.7 1.0 %copy-start.7 = (bf16[384,384]{1,0:T(8,128)(2,1)S(1)}, bf16[384,384]{1,0:T(8,128)(2,1)}, u32[]{:S(2)}) copy-start(bf16[384,384]{1,0:T(8,128)(2,1)} %copy-done.6) | copy-start | bytes 884740
  48.7 1.0 %copy-start.9 = (bf16[384,384]{1,0:T(8,128)(2,1)S(1)}, bf16[384,384]{1,0:T(8,128)(2,1)}, u32[]{:S(2)}) copy-start(bf16[384,384]{1,0:T(8,128)(2,1)} %copy-done.8) | copy-start | bytes 884740
  49.7 1.0 %copy-start.11 = (bf16[384,384]{1,0:T(8,128)(2,1)S(1)}, bf16[384,384]{1,0:T(8,128)(2,1)}, u32[]{:S(2)}) copy-start(bf16[384,384]{1,0:T(8,128)(2,1)} %copy-done.10) | copy-start | bytes 884740
  50.6 1.0 %copy-start.13 = (bf16[384,384]{1,0:T(8,128)(2,1)S(1)}, bf16[384,384]{1,0:T(8,128)(2,1)}, u32[]{:S(2)}) copy-start(bf16[384,384]{1,0:T(8,128)(2,1)} %copy-done.12) | copy-start | bytes 884740
  51.6 1.0 %copy-start.15 = (bf16[384,384]{1,0:T(8,128)(2,1)S(1)}, bf16[384,384]{1,0:T(8,128)(2,1)}, u32[]{:S(2)}) copy-start(bf16[384,384]{1,0:T(8,128)(2,1)} %copy-done.14) | copy-start | bytes 884740
  (1 other events, 0.7 us)

commit v3 on v2

--- a/solution.py
+++ b/solution.py
@@ -13,6 +13,8 @@
 FLOOR = -1e30
 BLOCK = 128
 LOG2_3 = 1.584962500721156
+LONG = 20_000_000_000
+SHORT = 1000
 
 
 def moved(block, pairs):
@@ -50,7 +52,7 @@
             for part, buf in enumerate((key_buf, value_buf)):
                 copies.append(
                     pltpu.make_async_copy(
-                        frames[f][2 * half + part],
+                        frames[f][2 * half + part].at[pl.ds(0, queries), :],
                         buf.at[f, pl.ds(half * queries, queries), :],
                         sems.at[f, half, part],
                     )
@@ -157,19 +159,18 @@
             outs[i][1][...] = stat
 
 
-def attend(plan, windows, mem_index, valids, queries, frames, states, finish, width):
+def attend(plan, windows, mem_index, valids, queries, frames, states, finish, width, cost):
     n_q, n_f = len(queries), len(frames)
     tokens, channels = queries[0].shape
     heads = channels // HEAD_DIM
     scalars = pl.BlockSpec(memory_space=pltpu.SMEM)
-    anywhere = pl.BlockSpec(memory_space=pltpu.HBM)
     whole = pl.BlockSpec(memory_space=pltpu.VMEM)
     fresh = tuple(s is None for s in states)
     operands = [mem_index, *valids, *queries]
-    specs = [scalars] * (1 + n_q) + [anywhere] * n_q
+    specs = [scalars] * (1 + n_q) + [whole] * n_q
     for frame in frames:
         operands += frame
-        specs += [anywhere] * 4
+        specs += [whole] * 4
     for state in states:
         if state is not None:
             operands += state
@@ -196,12 +197,8 @@
             pltpu.VMEM((n_q, heads, tokens, HEAD_DIM), jnp.float32),
             pltpu.SemaphoreType.DMA((n_f + n_q, 2, 2)),
         ],
-        compiler_params=pltpu.CompilerParams(vmem_limit_bytes=32 << 20),
-        cost_estimate=pl.CostEstimate(
-            flops=n_q * n_f * 8 * tokens * tokens * channels,
-            transcendentals=n_q * n_f * 2 * tokens * tokens * heads,
-            bytes_accessed=(n_f * 4 + n_q * 6) * tokens * channels * 2,
-        ),
+        compiler_params=pltpu.CompilerParams(vmem_limit_bytes=16 << 20),
+        cost_estimate=pl.CostEstimate(flops=cost, transcendentals=0, bytes_accessed=1000),
     )(*operands)
     outs = list(outs)
     return [outs.pop(0) if done else (outs.pop(0), outs.pop(0)) for done in finish]
@@ -247,16 +244,31 @@
     query, key, value = flat(queries), flat(keys), flat(values)
     inward = [(0, 1), (3, 2)]
     across = [(1, 2), (2, 1)]
-    end_key, end_value = moved(key, inward), moved(value, inward)
-    mid = with_other_half(moved(key, across), moved(value, across))
-    own = with_other_half(key, value)
-    end_key, end_value, late_query = lax.optimization_barrier((end_key, end_value, query))
-    far_key, far_value = moved(end_key, across), moved(end_value, across)
     marks = jnp.broadcast_to(valid_prev[0][:, None], (shape[1], shape[3])).astype(jnp.bfloat16)
     marks = jnp.pad(marks, ((0, 16 - shape[1]), (0, 0)))
-    end_query = moved(jnp.concatenate([late_query, marks], 0), inward)
-    end_valid = end_query[tokens : tokens + shape[1], 0].astype(jnp.int32)[None]
-    end_query = end_query[:tokens]
+    end_key = moved(key, inward)
+    end_value = moved(jnp.concatenate([value, marks], 0), inward)
+    mid_key, mid_value = moved(key, across), moved(value, across)
+    end_query = moved(query, inward)
+    own = with_other_half(key, value)
+    far_key, far_value = moved(end_key, across), moved(end_value, across)
+    end_valid = end_value[tokens : tokens + shape[1], 0].astype(jnp.int32)[None]
+    (state,) = attend(
+        functools.partial(plan_four, (0,), (0,)),
+        False,
+        mem_index,
+        [valid_prev],
+        [query],
+        [own],
+        [None],
+        [False],
+        width,
+        LONG,
+    )
+    mid_key, mid_value, end_key, end_value, state = lax.optimization_barrier(
+        (mid_key, mid_value, end_key, end_value, state)
+    )
+    mid = with_other_half(mid_key, mid_value)
     end = with_other_half(end_key, end_value)
     (end_state,) = attend(
         functools.partial(plan_four, (1,), (0, 1, 2)),
@@ -268,6 +280,7 @@
         [None],
         [False],
         width,
+        SHORT,
     )
     far_key, far_value, end_state = lax.optimization_barrier((far_key, far_value, end_state))
     far = with_other_half(far_key, far_value)
@@ -281,18 +294,20 @@
         [end_state],
         [True],
         width,
+        SHORT,
     )
     back = moved(end_out, [(1, 0), (2, 3)])
     (out,) = attend(
-        functools.partial(plan_four, (0,), (0, 1, 2, 3)),
+        functools.partial(plan_four, (0,), (1, 2, 3)),
         True,
         mem_index,
         [valid_prev],
         [query],
-        [own, mid, end, far],
-        [None],
+        [mid, end, far],
+        [state],
         [True],
         width,
+        LONG,
     )
     z = lax.axis_index("frame")
     return jnp.where((z == 1) | (z == 2), out, back).reshape(shape)
@@ -320,7 +335,7 @@
         with_other_half(memory[1, 0], memory[1, 1]),
     ]
     (out,) = attend(
-        plan_any, True, mem_index, [valid_prev], [flat(queries)], frames, [None], [True], width
+        plan_any, True, mem_index, [valid_prev], [flat(queries)], frames, [None], [True], width, LONG
     )
     return out.reshape(shape)
 

time: 60.7 us -> 56.5 us (0.931)
  the two profiles are of different devices: /device:TPU:23 before, /device:TPU:0 now
where the time goes in v3:
time: 56.5 us; the launch traced here: 57 us
  waiting for transfers between devices  26.4 us (47%)
  starting transfers between devices  18.4 us (33%)
  Pallas kernels  7.41 us (13%)
  local copies, waits for them, and re-layouts  2.5 us (4%)
  other arithmetic  2.03 us (4%)
    ppermute x8, waiting for transfers between devices, moved(): return lax.ppermute(block, 'frame', pairs)  24.4 us
    ppermute x8, starting transfers between devices, moved(): return lax.ppermute(block, 'frame', pairs)  16.6 us
    pallas_call x4, Pallas kernels, attend(): pl.pallas_call(functools.partial(attend_kernel, plan, n_q, n_f, fresh, tu...  7.41 us
    unnamed x28, local copies, waits for them, and re-layouts  2.5 us
    ppermute x8, waiting for transfers between devices, swapped(): return lax.ppermute(block, 'row', [(0, 1), (1, 0)])  1.97 us
    ppermute x8, starting transfers between devices, swapped(): return lax.ppermute(block, 'row', [(0, 1), (1, 0)])  1.79 us
    concatenate x2, other arithmetic, four_frames(): end_value = moved(jnp.concatenate([value, marks], 0), inward)  1.15 us
  transfers between devices with their start and end apart: 16, of which 5 were waited for; matrix products, arithmetic and copies ran while one was open for 2% of the time, Pallas kernels for 10%

profile of v3, /device:TPU:0, one launch (start us, length us, event | category | flops | bytes accessed | tf_op | source)
XLA Modules:
  0.0 57.0 jit_solution(4698539531612305799)
XLA Ops:
  0.0 0.5 collective-permute-start.4
  0.5 4.6 %collective-permute-start.2 = (bf16[384,384]{1,0:T(8,128)(2,1)}, bf16[384,384]{1,0:T(8,128)(2,1)S(1)}, u32[]{:S(2)}, u32[]{:S(2)}) collective-permute-start(bf16[384,384]{1,0:T(8,128)(2,1)} %bitcast.13), channel_id=1, source_target_pairs={{0,4},{12,8},{1,5},{13,9},{2,6},{14,10},{3,7},{15,11},{16,20},{28,... | collective-permute-start | bytes 884744 | tf_op jit(solution)/shard_map/ppermute | solution.py:21
  5.1 0.7 %collective-permute-start = (bf16[384,384]{1,0:T(8,128)(2,1)}, bf16[384,384]{1,0:T(8,128)(2,1)S(1)}, u32[]{:S(2)}, u32[]{:S(2)}) collective-permute-start(bf16[384,384]{1,0:T(8,128)(2,1)} %bitcast.14), channel_id=1, source_target_pairs={{4,8},{8,4},{5,9},{9,5},{6,10},{10,6},{7,11},{11,7},{20,24},{24,20... | collective-permute-start | bytes 884744 | tf_op jit(solution)/shard_map/ppermute | solution.py:21
  5.8 0.1 collective-permute-start.5
  5.9 0.7 %collective-permute-start.1 = (bf16[384,384]{1,0:T(8,128)(2,1)}, bf16[384,384]{1,0:T(8,128)(2,1)S(1)}, u32[]{:S(2)}, u32[]{:S(2)}) collective-permute-start(bf16[384,384]{1,0:T(8,128)(2,1)} %bitcast.8), channel_id=1, source_target_pairs={{4,8},{8,4},{5,9},{9,5},{6,10},{10,6},{7,11},{11,7},{20,24},{24,20... | collective-permute-start | bytes 884744 | tf_op jit(solution)/shard_map/ppermute | solution.py:21
  6.6 0.0 copy-start
  6.7 0.0 copy-start.1
  6.7 1.1 %pad_maximum_fusion = bf16[400,384]{1,0:T(8,128)(2,1)S(1)} fusion(bf16[384,384]{1,0:T(8,128)(2,1)} %bitcast.9, bf16[400]{0:T(512)(128)(2,1)S(1)} %fusion), kind=kLoop, calls=%fused_computation | loop fusion | flops 614400 | bytes 602912 | tf_op jit(solution)/shard_map/concatenate | solution.py:250
  7.8 0.0 copy-start.6
  7.8 5.8 %collective-permute-start.3 = (bf16[400,384]{1,0:T(8,128)(2,1)S(1)}, bf16[400,384]{1,0:T(8,128)(2,1)S(1)}, u32[]{:S(2)}, u32[]{:S(2)}) collective-permute-start(bf16[400,384]{1,0:T(8,128)(2,1)S(1)} %pad_maximum_fusion), channel_id=1, source_target_pairs={{0,4},{12,8},{1,5},{13,9},{2,6},{14,10},{3,7},{15,11},{16,20},{28,... | collective-permute-start | bytes 921608 | tf_op jit(solution)/shard_map/ppermute | solution.py:21
  13.6 1.3 %collective-permute-start.12 = (bf16[384,384]{1,0:T(8,128)(2,1)}, bf16[384,384]{1,0:T(8,128)(2,1)S(1)}, u32[]{:S(2)}, u32[]{:S(2)}) collective-permute-start(bf16[384,384]{1,0:T(8,128)(2,1)} %bitcast.19), channel_id=1, source_target_pairs={{0,4},{12,8},{1,5},{13,9},{2,6},{14,10},{3,7},{15,11},{16,20},{28,... | collective-permute-start | bytes 884744 | tf_op jit(solution)/shard_map/ppermute | solution.py:21
  15.0 1.0 %copy-done.7 = bf16[1,8,48,384]{3,2,1,0:T(8,128)(2,1)S(1)} copy-done((bf16[1,8,48,384]{3,2,1,0:T(8,128)(2,1)S(1)}, bf16[1,8,48,384]{3,2,1,0:T(8,128)(2,1)}, u32[]{:S(2)}) %copy-start.7) | copy-done | bytes 294936
  16.0 1.1 %shard_map.55 = (f32[384,384]{1,0:T(8,128)S(1)}, f32[384,128]{1,0:T(8,128)S(1)}) custom-call(s32[2]{0:T(128)S(1)} %copy-done.6, s32[1,8]{1,0:T(1,128)S(1)} %copy-done.9, bf16[384,384]{1,0:T(8,128)(2,1)S(1)} %bitcast.20, bf16[384,384]{1,0:T(8,128)(2,1)S(1)} %bitcast.15, bf16[384,384]{1,0:T(8,128)(2,1)S(1)} %bitcast.10, ...), custom_call_target="tpu_custom_call" | custom-call | flops 20000000000 | bytes 1000 | tf_op jit(solution)/shard_map/pallas_call | solution.py:185
  17.1 0.8 %copy-done.10 = f32[384,384]{1,0:T(8,128)} copy-done((f32[384,384]{1,0:T(8,128)}, f32[384,384]{1,0:T(8,128)S(1)}, u32[]{:S(2)}) %copy-start.10) | copy-done | bytes 589848
  17.9 0.7 %copy-done.12 = f32[384,128]{1,0:T(8,128)} copy-done((f32[384,128]{1,0:T(8,128)}, f32[384,128]{1,0:T(8,128)S(1)}, u32[]{:S(2)}) %copy-start.12) | copy-done | bytes 196632
  18.6 2.6 %collective-permute-done.3.refs_12_.refs_8_ = bf16[400,384]{1,0:T(8,128)(2,1)S(1)} collective-permute-done((bf16[400,384]{1,0:T(8,128)(2,1)S(1)}, bf16[400,384]{1,0:T(8,128)(2,1)S(1)}, u32[]{:S(2)}, u32[]{:S(2)}) %collective-permute-start.3) | collective-permute-done | bytes 307232 | tf_op jit(solution)/shard_map/ppermute | solution.py:21
  21.2 0.5 collective-permute-start.9
  21.7 0.7 %collective-permute-start.11 = (bf16[400,384]{1,0:T(8,128)(2,1)S(1)}, bf16[400,384]{1,0:T(8,128)(2,1)S(1)}, u32[]{:S(2)}, u32[]{:S(2)}) collective-permute-start(bf16[400,384]{1,0:T(8,128)(2,1)S(1)} %collective-permute-done.3.refs_12_.refs_8_), channel_id=1, source_target_pairs={{4,8},{8,4},{5,9},{9,5},{6,10},{10,6},{7,11},{11,7},{20,24},{24,20... | collective-permute-start | bytes 921608 | tf_op jit(solution)/shard_map/ppermute | solution.py:21
  22.4 0.1 collective-permute-start.7
  22.5 4.4 %collective-permute-done.12.refs_2_ = bf16[384,384]{1,0:T(8,128)(2,1)S(1)} collective-permute-done((bf16[384,384]{1,0:T(8,128)(2,1)}, bf16[384,384]{1,0:T(8,128)(2,1)S(1)}, u32[]{:S(2)}, u32[]{:S(2)}) %collective-permute-start.12) | collective-permute-done | bytes 294944 | tf_op jit(solution)/shard_map/ppermute | solution.py:21
  26.9 1.4 %collective-permute-start.10 = (bf16[384,384]{1,0:T(8,128)(2,1)S(1)}, bf16[384,384]{1,0:T(8,128)(2,1)}, u32[]{:S(2)}, u32[]{:S(2)}) collective-permute-start(bf16[384,384]{1,0:T(8,128)(2,1)S(1)} %collective-permute-done.2.refs_11_.refs_7_), channel_id=1, source_target_pairs={{4,8},{8,4},{5,9},{9,5},{6,10},{10,6},{7,11},{11,7},{20,24},{24,20... | collective-permute-start | bytes 884744 | tf_op jit(solution)/shard_map/ppermute | solution.py:21
  28.2 0.1 convert_reduce_fusion
  28.4 0.1 collective-permute-done.8.refs_13_.refs_9_
  28.5 1.8 %shard_map.56 = (f32[384,384]{1,0:T(8,128)S(1)}, f32[384,128]{1,0:T(8,128)S(1)}) custom-call(s32[2]{0:T(128)S(1)} %copy-done.6, s32[1,8]{1,0:T(1,128)S(1)} %bitcast.17, bf16[384,384]{1,0:T(8,128)(2,1)S(1)} %collective-permute-done.12.refs_2_, bf16[384,384]{1,0:T(8,128)(2,1)S(1)} %bitcast.16, bf16[384,384]{1,0:T(8,128)(2,1)S(1)} %bitcast.11, ...), custom_call_target="tpu_custom_call" | custom-call | flops 1000 | bytes 1000 | tf_op jit(solution)/shard_map/pallas_call | solution.py:185
  30.3 0.5 collective-permute-start.14
  30.8 0.1 collective-permute-start.13
  30.9 1.9 %collective-permute-done.13.refs_13_.refs_5_ = bf16[384,384]{1,0:T(8,128)(2,1)} collective-permute-done((bf16[384,384]{1,0:T(8,128)(2,1)}, bf16[384,384]{1,0:T(8,128)(2,1)}, u32[]{:S(2)}, u32[]{:S(2)}) %collective-permute-start.13) | collective-permute-done | bytes 294944 | tf_op jit(solution)/shard_map/ppermute | solution.py:25
  32.8 1.9 %shard_map.58 = bf16[384,384]{1,0:T(8,128)(2,1)S(1)} custom-call(s32[2]{0:T(128)S(1)} %copy-done.6, s32[1,8]{1,0:T(1,128)S(1)} %bitcast.18, bf16[384,384]{1,0:T(8,128)(2,1)S(1)} %collective-permute-done.12.refs_2_, bf16[384,384]{1,0:T(8,128)(2,1)} %collective-permute-done.10.refs_11_.refs_3_, bf16[400,384]{1,0:T(8,128)(2,1)S(1)} %collective-permute-done.11.refs_12_.refs_4_, ...), custom_call_target="tpu_custom_call" | custom-call | flops 1000 | bytes 1000 | tf_op jit(solution)/shard_map/pallas_call | solution.py:185
  34.7 1.5 %collective-permute-start.15 = (bf16[384,384]{1,0:T(8,128)(2,1)S(1)}, bf16[384,384]{1,0:T(8,128)(2,1)S(1)}, u32[]{:S(2)}, u32[]{:S(2)}) collective-permute-start(bf16[384,384]{1,0:T(8,128)(2,1)S(1)} %shard_map.58), channel_id=1, source_target_pairs={{4,0},{8,12},{5,1},{9,13},{6,2},{10,14},{7,3},{11,15},{20,16},{24,... | collective-permute-start | bytes 884744 | tf_op jit(solution)/shard_map/ppermute | solution.py:21
  36.3 2.6 %shard_map.57 = bf16[384,384]{1,0:T(8,128)(2,1)S(1)} custom-call(s32[2]{0:T(128)S(1)} %copy-done.6, s32[1,8]{1,0:T(1,128)S(1)} %copy-done.9, bf16[384,384]{1,0:T(8,128)(2,1)S(1)} %bitcast.21, bf16[384,384]{1,0:T(8,128)(2,1)S(1)} %collective-permute-done.refs_7_.refs_3_, bf16[384,384]{1,0:T(8,128)(2,1)S(1)} %collective-permute-done.1.refs_8_.refs_4_, ...), custom_call_target="tpu_custom_call" | custom-call | flops 20000000000 | bytes 1000 | tf_op jit(solution)/shard_map/pallas_call | solution.py:185
  38.8 17.4 %collective-permute-done.15 = bf16[384,384]{1,0:T(8,128)(2,1)S(1)} collective-permute-done((bf16[384,384]{1,0:T(8,128)(2,1)S(1)}, bf16[384,384]{1,0:T(8,128)(2,1)S(1)}, u32[]{:S(2)}, u32[]{:S(2)}) %collective-permute-start.15) | collective-permute-done | bytes 294944 | tf_op jit(solution)/shard_map/ppermute | solution.py:21
  56.3 0.8 %broadcast_select_fusion = bf16[384,384]{1,0:T(8,128)(2,1)} fusion(bf16[384,384]{1,0:T(8,128)(2,1)S(1)} %shard_map.57, bf16[384,384]{1,0:T(8,128)(2,1)S(1)} %collective-permute-done.15, pred[]{:T(512)S(6)} %or.3), kind=kLoop, calls=%fused_computation.1 | loop fusion | flops 147456 | bytes 884737 | tf_op jit(solution)/shard_map/jit(_where)/select_n | solution.py:313
  (37 shorter events, 0.1 us)
Async XLA Ops:
  0.0 6.6 %copy-start.9 = (s32[1,8]{1,0:T(1,128)S(1)}, s32[1,8]{1,0:T(1,128)}, u32[]{:S(2)}) copy-start(s32[1,8]{1,0:T(1,128)} %refs_1_.3) | copy-start | bytes 100
  0.0 7.8 %collective-permute-start.4 = (bf16[384,384]{1,0:T(8,128)(2,1)}, bf16[384,384]{1,0:T(8,128)(2,1)S(1)}, u32[]{:S(2)}, u32[]{:S(2)}) collective-permute-start(bf16[384,384]{1,0:T(8,128)(2,1)} %bitcast.12), channel_id=1, source_target_pairs={{0,2},{2,0},{1,3},{3,1},{4,6},{6,4},{5,7},{7,5},{8,10},{10,8},{9,1... | collective-permute-start | bytes 884744 | tf_op jit(solution)/shard_map/ppermute | solution.py:25
  0.5 18.2 %collective-permute-start.2 = (bf16[384,384]{1,0:T(8,128)(2,1)}, bf16[384,384]{1,0:T(8,128)(2,1)S(1)}, u32[]{:S(2)}, u32[]{:S(2)}) collective-permute-start(bf16[384,384]{1,0:T(8,128)(2,1)} %bitcast.13), channel_id=1, source_target_pairs={{0,4},{12,8},{1,5},{13,9},{2,6},{14,10},{3,7},{15,11},{16,20},{28,... | collective-permute-start | bytes 884744 | tf_op jit(solution)/shard_map/ppermute | solution.py:21
  5.1 13.5 %collective-permute-start = (bf16[384,384]{1,0:T(8,128)(2,1)}, bf16[384,384]{1,0:T(8,128)(2,1)S(1)}, u32[]{:S(2)}, u32[]{:S(2)}) collective-permute-start(bf16[384,384]{1,0:T(8,128)(2,1)} %bitcast.14), channel_id=1, source_target_pairs={{4,8},{8,4},{5,9},{9,5},{6,10},{10,6},{7,11},{11,7},{20,24},{24,20... | collective-permute-start | bytes 884744 | tf_op jit(solution)/shard_map/ppermute | solution.py:21
  5.8 7.8 %collective-permute-start.5 = (bf16[384,384]{1,0:T(8,128)(2,1)}, bf16[384,384]{1,0:T(8,128)(2,1)S(1)}, u32[]{:S(2)}, u32[]{:S(2)}) collective-permute-start(bf16[384,384]{1,0:T(8,128)(2,1)} %bitcast.7), channel_id=1, source_target_pairs={{0,2},{2,0},{1,3},{3,1},{4,6},{6,4},{5,7},{7,5},{8,10},{10,8},{9,1... | collective-permute-start | bytes 884744 | tf_op jit(solution)/shard_map/ppermute | solution.py:25
  5.9 12.7 %collective-permute-start.1 = (bf16[384,384]{1,0:T(8,128)(2,1)}, bf16[384,384]{1,0:T(8,128)(2,1)S(1)}, u32[]{:S(2)}, u32[]{:S(2)}) collective-permute-start(bf16[384,384]{1,0:T(8,128)(2,1)} %bitcast.8), channel_id=1, source_target_pairs={{4,8},{8,4},{5,9},{9,5},{6,10},{10,6},{7,11},{11,7},{20,24},{24,20... | collective-permute-start | bytes 884744 | tf_op jit(solution)/shard_map/ppermute | solution.py:21
  6.6 8.3 %copy-start = (bf16[1,8,48,384]{3,2,1,0:T(8,128)(2,1)S(1)}, bf16[1,8,48,384]{3,2,1,0:T(8,128)(2,1)}, u32[]{:S(2)}) copy-start(bf16[1,8,48,384]{3,2,1,0:T(8,128)(2,1)} %param.7) | copy-start | bytes 884740
  6.7 8.3 %copy-start.1 = (bf16[1,8,48,384]{3,2,1,0:T(8,128)(2,1)S(1)}, bf16[1,8,48,384]{3,2,1,0:T(8,128)(2,1)}, u32[]{:S(2)}) copy-start(bf16[1,8,48,384]{3,2,1,0:T(8,128)(2,1)} %param.6) | copy-start | bytes 884740
  7.8 7.2 %copy-start.6 = (s32[2]{0:T(128)S(1)}, s32[2]{0:T(128)}, u32[]{:S(2)}) copy-start(s32[2]{0:T(128)} %refs_0_.7) | copy-start | bytes 28
  7.8 13.4 %collective-permute-start.3 = (bf16[400,384]{1,0:T(8,128)(2,1)S(1)}, bf16[400,384]{1,0:T(8,128)(2,1)S(1)}, u32[]{:S(2)}, u32[]{:S(2)}) collective-permute-start(bf16[400,384]{1,0:T(8,128)(2,1)S(1)} %pad_maximum_fusion), channel_id=1, source_target_pairs={{0,4},{12,8},{1,5},{13,9},{2,6},{14,10},{3,7},{15,11},{16,20},{28,... | collective-permute-start | bytes 921608 | tf_op jit(solution)/shard_map/ppermute | solution.py:21
  13.6 13.2 %collective-permute-start.12 = (bf16[384,384]{1,0:T(8,128)(2,1)}, bf16[384,384]{1,0:T(8,128)(2,1)S(1)}, u32[]{:S(2)}, u32[]{:S(2)}) collective-permute-start(bf16[384,384]{1,0:T(8,128)(2,1)} %bitcast.19), channel_id=1, source_target_pairs={{0,4},{12,8},{1,5},{13,9},{2,6},{14,10},{3,7},{15,11},{16,20},{28,... | collective-permute-start | bytes 884744 | tf_op jit(solution)/shard_map/ppermute | solution.py:21
  15.0 1.0 %copy-start.7 = (bf16[1,8,48,384]{3,2,1,0:T(8,128)(2,1)S(1)}, bf16[1,8,48,384]{3,2,1,0:T(8,128)(2,1)}, u32[]{:S(2)}) copy-start(bf16[1,8,48,384]{3,2,1,0:T(8,128)(2,1)} %param.5) | copy-start | bytes 884740
  17.1 0.8 %copy-start.10 = (f32[384,384]{1,0:T(8,128)}, f32[384,384]{1,0:T(8,128)S(1)}, u32[]{:S(2)}) copy-start(f32[384,384]{1,0:T(8,128)S(1)} %get-tuple-element.29.refs_15_) | copy-start | bytes 1769476
  17.9 0.7 %copy-start.12 = (f32[384,128]{1,0:T(8,128)}, f32[384,128]{1,0:T(8,128)S(1)}, u32[]{:S(2)}) copy-start(f32[384,128]{1,0:T(8,128)S(1)} %get-tuple-element.30.refs_16_) | copy-start | bytes 589828
  21.2 5.6 %collective-permute-start.6 = (bf16[384,384]{1,0:T(8,128)(2,1)S(1)}, bf16[384,384]{1,0:T(8,128)(2,1)S(1)}, u32[]{:S(2)}, u32[]{:S(2)}) collective-permute-start(bf16[384,384]{1,0:T(8,128)(2,1)S(1)} %collective-permute-done.refs_7_.refs_3_), channel_id=1, source_target_pairs={{0,2},{2,0},{1,3},{3,1},{4,6},{6,4},{5,7},{7,5},{8,10},{10,8},{9,1... | collective-permute-start | bytes 884744 | tf_op jit(solution)/shard_map/ppermute | solution.py:25
  21.2 7.2 %collective-permute-start.9 = (bf16[400,384]{1,0:T(8,128)(2,1)S(1)}, bf16[400,384]{1,0:T(8,128)(2,1)S(1)}, u32[]{:S(2)}, u32[]{:S(2)}) collective-permute-start(bf16[400,384]{1,0:T(8,128)(2,1)S(1)} %collective-permute-done.3.refs_12_.refs_8_), channel_id=1, source_target_pairs={{0,2},{2,0},{1,3},{3,1},{4,6},{6,4},{5,7},{7,5},{8,10},{10,8},{9,1... | collective-permute-start | bytes 921608 | tf_op jit(solution)/shard_map/ppermute | solution.py:25
  21.7 8.5 %collective-permute-start.11 = (bf16[400,384]{1,0:T(8,128)(2,1)S(1)}, bf16[400,384]{1,0:T(8,128)(2,1)S(1)}, u32[]{:S(2)}, u32[]{:S(2)}) collective-permute-start(bf16[400,384]{1,0:T(8,128)(2,1)S(1)} %collective-permute-done.3.refs_12_.refs_8_), channel_id=1, source_target_pairs={{4,8},{8,4},{5,9},{9,5},{6,10},{10,6},{7,11},{11,7},{20,24},{24,20... | collective-permute-start | bytes 921608 | tf_op jit(solution)/shard_map/ppermute | solution.py:21
  22.4 6.0 %collective-permute-start.7 = (bf16[384,384]{1,0:T(8,128)(2,1)S(1)}, bf16[384,384]{1,0:T(8,128)(2,1)S(1)}, u32[]{:S(2)}, u32[]{:S(2)}) collective-permute-start(bf16[384,384]{1,0:T(8,128)(2,1)S(1)} %collective-permute-done.1.refs_8_.refs_4_), channel_id=1, source_target_pairs={{0,2},{2,0},{1,3},{3,1},{4,6},{6,4},{5,7},{7,5},{8,10},{10,8},{9,1... | collective-permute-start | bytes 884744 | tf_op jit(solution)/shard_map/ppermute | solution.py:25
  26.9 1.6 %collective-permute-start.8 = (bf16[384,384]{1,0:T(8,128)(2,1)S(1)}, bf16[384,384]{1,0:T(8,128)(2,1)S(1)}, u32[]{:S(2)}, u32[]{:S(2)}) collective-permute-start(bf16[384,384]{1,0:T(8,128)(2,1)S(1)} %collective-permute-done.2.refs_11_.refs_7_), channel_id=1, source_target_pairs={{0,2},{2,0},{1,3},{3,1},{4,6},{6,4},{5,7},{7,5},{8,10},{10,8},{9,1... | collective-permute-start | bytes 884744 | tf_op jit(solution)/shard_map/ppermute | solution.py:25
  26.9 3.4 %collective-permute-start.10 = (bf16[384,384]{1,0:T(8,128)(2,1)S(1)}, bf16[384,384]{1,0:T(8,128)(2,1)}, u32[]{:S(2)}, u32[]{:S(2)}) collective-permute-start(bf16[384,384]{1,0:T(8,128)(2,1)S(1)} %collective-permute-done.2.refs_11_.refs_7_), channel_id=1, source_target_pairs={{4,8},{8,4},{5,9},{9,5},{6,10},{10,6},{7,11},{11,7},{20,24},{24,20... | collective-permute-start | bytes 884744 | tf_op jit(solution)/shard_map/ppermute | solution.py:21
  28.4 1.9 %copy-start.2 = (bf16[384,384]{1,0:T(8,128)(2,1)}, bf16[384,384]{1,0:T(8,128)(2,1)S(1)}, u32[]{:S(2)}) copy-start(bf16[384,384]{1,0:T(8,128)(2,1)S(1)} %collective-permute-done.7.refs_10_.refs_6_) | copy-start | bytes 884740
  28.4 1.8 %copy-start.4 = (bf16[384,384]{1,0:T(8,128)(2,1)}, bf16[384,384]{1,0:T(8,128)(2,1)S(1)}, u32[]{:S(2)}) copy-start(bf16[384,384]{1,0:T(8,128)(2,1)S(1)} %collective-permute-done.8.refs_13_.refs_9_) | copy-start | bytes 884740
  30.3 2.5 %collective-permute-start.14 = (bf16[400,384]{1,0:T(8,128)(2,1)S(1)}, bf16[400,384]{1,0:T(8,128)(2,1)S(1)}, u32[]{:S(2)}, u32[]{:S(2)}) collective-permute-start(bf16[400,384]{1,0:T(8,128)(2,1)S(1)} %collective-permute-done.11.refs_12_.refs_4_), channel_id=1, source_target_pairs={{0,2},{2,0},{1,3},{3,1},{4,6},{6,4},{5,7},{7,5},{8,10},{10,8},{9,1... | collective-permute-start | bytes 921608 | tf_op jit(solution)/shard_map/ppermute | solution.py:25
  30.8 2.0 %collective-permute-start.13 = (bf16[384,384]{1,0:T(8,128)(2,1)}, bf16[384,384]{1,0:T(8,128)(2,1)}, u32[]{:S(2)}, u32[]{:S(2)}) collective-permute-start(bf16[384,384]{1,0:T(8,128)(2,1)} %collective-permute-done.10.refs_11_.refs_3_), channel_id=1, source_target_pairs={{0,2},{2,0},{1,3},{3,1},{4,6},{6,4},{5,7},{7,5},{8,10},{10,8},{9,1... | collective-permute-start | bytes 884744 | tf_op jit(solution)/shard_map/ppermute | solution.py:25
  30.9 5.3 %copy-start.3 = (bf16[384,384]{1,0:T(8,128)(2,1)S(1)}, bf16[384,384]{1,0:T(8,128)(2,1)}, u32[]{:S(2)}) copy-start(bf16[384,384]{1,0:T(8,128)(2,1)} %copy-done.2) | copy-start | bytes 884740
  30.9 5.3 %copy-start.5 = (bf16[384,384]{1,0:T(8,128)(2,1)S(1)}, bf16[384,384]{1,0:T(8,128)(2,1)}, u32[]{:S(2)}) copy-start(bf16[384,384]{1,0:T(8,128)(2,1)} %copy-done.4) | copy-start | bytes 884740
  30.9 5.3 %copy-start.8 = (bf16[1,8,48,384]{3,2,1,0:T(8,128)(2,1)S(1)}, bf16[1,8,48,384]{3,2,1,0:T(8,128)(2,1)}, u32[]{:S(2)}) copy-start(bf16[1,8,48,384]{3,2,1,0:T(8,128)(2,1)} %param.5) | copy-start | bytes 884740
  30.9 5.3 %copy-start.11 = (f32[384,384]{1,0:T(8,128)S(1)}, f32[384,384]{1,0:T(8,128)}, u32[]{:S(2)}) copy-start(f32[384,384]{1,0:T(8,128)} %copy-done.10) | copy-start | bytes 1769476
  30.9 5.3 %copy-start.13 = (f32[384,128]{1,0:T(8,128)S(1)}, f32[384,128]{1,0:T(8,128)}, u32[]{:S(2)}) copy-start(f32[384,128]{1,0:T(8,128)} %copy-done.12) | copy-start | bytes 589828
  34.7 21.5 %collective-permute-start.15 = (bf16[384,384]{1,0:T(8,128)(2,1)S(1)}, bf16[384,384]{1,0:T(8,128)(2,1)S(1)}, u32[]{:S(2)}, u32[]{:S(2)}) collective-permute-start(bf16[384,384]{1,0:T(8,128)(2,1)S(1)} %shard_map.58), channel_id=1, source_target_pairs={{4,0},{8,12},{5,1},{9,13},{6,2},{10,14},{7,3},{11,15},{20,16},{24,... | collective-permute-start | bytes 884744 | tf_op jit(solution)/shard_map/ppermute | solution.py:21
